TPU v7x, 32 devices: a whole 2x2x4 slice. The times are simulated.
32 devices in a mesh: groups: 2 (over x), tr: 16 (over z, y, core).
Axes of the slice: x: 2, y: 2, z: 4, core: 2. Of those that a mesh axis runs over, the one named last changes fastest.
Arguments:
- object_field: float32 [2, 16384, 1024], P(None, ('groups', 'tr')), parts along dimension 1, may hold values from -6 to 6
- probe_modes: float32 [2, 2, 256, 256], replicated, may hold values from -96 to 96
- scan_offsets: int32 [32, 8, 2], P(('groups', 'tr')), parts along dimension 0, may hold values from 0 to 768, as said below
- scan_counts: int32 [32], P(('groups', 'tr')), parts along dimension 0, may hold values from 1 to 8, as said below
- measured: int32 [32, 8, 256, 256], P(('groups', 'tr')), parts along dimension 0, may hold values from 0 to 4096
Outputs:
- object_grad: float32 [2, 16384, 1024], P(None, ('groups', 'tr')), parts along dimension 1
- probe_grad: float32 [2048, 256], P(('groups', 'tr')), parts along dimension 0
There are 2 independent parts, one for each index of `groups`. A program takes and returns all parts, laid end to end along the dimension named above; an argument that names none is the same for every part. Nothing has to cross between parts.
Inputs may be any that keep to these rules, and one draw needn't show every extreme that they name: `scan_counts`: each tile has 1 to 8 used scan positions, and some tile has exactly 8. `scan_offsets`: row offsets lie in 0 to 511 within the tile, column offsets in 0 to 768; both ends are reached; every slot holds a valid offset, used or not.
All inputs are finite; a program needn't handle non-finite values.
Results may differ from a plain program's by a relative error of at most 0.0095.
Values may be sent and summed in bfloat16 or wider, within the bound.
No kernel may reach another device: no remote copies, remote signals or barrier semaphores. Data moves between devices by JAX's collectives and lax.ppermute only.
A program may use at most 64 MiB of HBM per device.

v0:
```python
import jax
import jax.numpy as jnp
from jax import lax
from jax.sharding import PartitionSpec as P

loss_scale = 1.0 / 1024.0


def shifted(value, axis, steps):
    count = lax.axis_size(axis)
    initial, last = (max(0, -steps), min(count, count - steps))
    return lax.ppermute(value, axis, [(source, source + steps) for source in range(initial, last)])


def dft_table(patch_size):
    index_run = jnp.arange(patch_size, dtype=jnp.int32)
    product = index_run[:, None] * index_run[None, :] % patch_size
    phase_angle = -2.0 * jnp.pi / patch_size * product.astype(jnp.float32)
    unit_scale = 1.0 / jnp.sqrt(jnp.float32(patch_size))
    table_real = jnp.cos(phase_angle) * unit_scale
    table_imag = jnp.sin(phase_angle) * unit_scale
    upper_rows = jnp.concatenate([table_real, table_imag], axis=1)
    lower_rows = jnp.concatenate([-table_imag, table_real], axis=1)
    return jnp.concatenate([upper_rows, lower_rows], axis=0).astype(jnp.bfloat16)


def forward_part(patch, sqrt_counts, probe_modes, dft_matrix):
    patch_size = patch.shape[-1]
    mode_count = probe_modes.shape[0]
    probe_real = probe_modes[:, 0]
    probe_imag = probe_modes[:, 1]
    object_real = patch[0]
    object_imag = patch[1]
    exit_real = probe_real * object_real - probe_imag * object_imag
    exit_imag = probe_real * object_imag + probe_imag * object_real
    exit_wave = jnp.concatenate([exit_real, exit_imag], axis=-1).astype(jnp.bfloat16)
    half_done = jnp.einsum(
        "mpk,kl->mpl", exit_wave, dft_matrix, preferred_element_type=jnp.float32
    ).astype(jnp.bfloat16)
    stacked = jnp.concatenate([half_done[..., :patch_size], half_done[..., patch_size:]], axis=1)
    far_field = jnp.einsum("kq,mkp->mqp", dft_matrix, stacked, preferred_element_type=jnp.float32)
    far_real = far_field[:, :patch_size]
    far_imag = far_field[:, patch_size:]
    model_power = jnp.sum(far_real * far_real + far_imag * far_imag, axis=0)
    factor = 2.0 * loss_scale * (1.0 - sqrt_counts / jnp.sqrt(model_power + 1.0))
    return (
        (far_field.reshape(mode_count, 2, patch_size, patch_size) * factor)
        .reshape(mode_count, 2 * patch_size, patch_size)
        .astype(jnp.bfloat16)
    )


def backward_part(grad_far, patch, probe_modes, dft_matrix):
    patch_size = patch.shape[-1]
    probe_real = probe_modes[:, 0]
    probe_imag = probe_modes[:, 1]
    object_real = patch[0]
    object_imag = patch[1]
    back_rows = jnp.einsum(
        "qk,mkp->mqp", dft_matrix, grad_far, preferred_element_type=jnp.float32
    ).astype(jnp.bfloat16)
    col_major = jnp.concatenate([back_rows[:, :patch_size], back_rows[:, patch_size:]], axis=-1)
    grad_wave = jnp.einsum("mpk,lk->mpl", col_major, dft_matrix, preferred_element_type=jnp.float32)
    grad_real = grad_wave[..., :patch_size]
    grad_imag = grad_wave[..., patch_size:]
    obj_real = jnp.sum(probe_real * grad_real + probe_imag * grad_imag, axis=0)
    obj_imag = jnp.sum(probe_real * grad_imag - probe_imag * grad_real, axis=0)
    probe_greal = object_real * grad_real + object_imag * grad_imag
    probe_gimag = object_real * grad_imag - object_imag * grad_real
    return (jnp.stack([obj_real, obj_imag]), jnp.stack([probe_greal, probe_gimag], axis=1))


def patch_grads(patch, sqrt_counts, probe_modes, dft_matrix):
    grad_far = forward_part(patch, sqrt_counts, probe_modes, dft_matrix)
    return backward_part(grad_far, patch, probe_modes, dft_matrix)


def add_block(gradient, block, offset_pair):
    corner = (jnp.int32(0), offset_pair[0], offset_pair[1])
    current = lax.dynamic_slice(gradient, corner, block.shape)
    return lax.dynamic_update_slice(gradient, current + block, corner)


def on_device(object_field, probe_modes, scan_offsets, scan_counts, measured):
    patch_size = probe_modes.shape[-1]
    strip_rows = object_field.shape[1]
    dft_matrix = dft_table(patch_size)
    lower_band = shifted(object_field[:, :patch_size, :], "tr", -1)
    extended = jnp.concatenate([object_field, lower_band], axis=1)
    sqrt_counts = jnp.sqrt(measured[0].astype(jnp.float32))
    offsets = scan_offsets[0]
    own_count = scan_counts[0]

    def extract_patch(offset_pair):
        return lax.dynamic_slice(
            extended, (jnp.int32(0), offset_pair[0], offset_pair[1]), (2, patch_size, patch_size)
        )

    def local_slot(slot_index, loop_state):
        gradient, probe_sum = loop_state
        offset_pair = offsets[slot_index]
        part_object, part_probe = patch_grads(
            extract_patch(offset_pair), sqrt_counts[slot_index], probe_modes, dft_matrix
        )
        return (add_block(gradient, part_object, offset_pair), probe_sum + part_probe)

    zero_grad = jnp.zeros(extended.shape, jnp.float32)
    zero_probe = jnp.zeros(probe_modes.shape, jnp.float32)
    gradient, probe_sum = lax.fori_loop(
        jnp.int32(0), own_count, local_slot, (zero_grad, zero_probe)
    )
    edge_grad = shifted(gradient[:, strip_rows:, :], "tr", 1)
    object_grad = gradient[:, :strip_rows, :] + jnp.pad(
        edge_grad, ((0, 0), (0, strip_rows - patch_size), (0, 0))
    )
    flat_probe = probe_sum.reshape(-1, patch_size)
    whole_probe = lax.psum(flat_probe, "tr")
    share_rows = flat_probe.shape[0] // lax.axis_size("tr")
    probe_grad = lax.dynamic_slice_in_dim(
        whole_probe, lax.axis_index("tr") * share_rows, share_rows, 0
    )
    return (object_grad, probe_grad)


def solution(mesh):
    return jax.shard_map(
        on_device,
        mesh=mesh,
        in_specs=(
            P(None, ("groups", "tr"), None),
            P(),
            P(("groups", "tr"), None, None),
            P(("groups", "tr")),
            P(("groups", "tr"), None, None, None),
        ),
        out_specs=(P(None, ("groups", "tr"), None), P(("groups", "tr"), None)),
        check_vma=False,
    )
```

profile of v0, /device:TPU:13, one launch (start us, length us, event | category | flops | bytes accessed | tf_op | source)
XLA Modules:
  0.0 307.8 jit_solution(7520786833410476199)
XLA Ops:
  7.2 3.2 %slice.59 = f32[2,256,1024]{2,1,0:T(8,128)} slice(f32[2,512,1024]{2,1,0:T(8,128)} %param.7), slice={[0:2], [0:256], [0:1024]} | slice | bytes 4194304 | tf_op jit(solution)/shard_map/slice | solution.py:88
  10.5 2.6 collective-permute-start
  13.1 2.9 copy.9
  16.1 1.0 fusion.37
  17.0 1.1 negate_convert_fusion
  18.2 3.5 %sqrt_bitcast_fusion = f32[8,256,256]{1,2,0:T(8,128)} fusion(s32[1,8,256,256]{2,3,1,0:T(8,128)} %copy.9), kind=kLoop, calls=%fused_computation.55 | loop fusion | flops 524288 | bytes 4194304 | tf_op jit(solution)/shard_map/sqrt | solution.py:90
  21.7 17.3 %collective-permute-done = f32[2,256,1024]{2,1,0:T(8,128)} collective-permute-done((f32[2,256,1024]{2,1,0:T(8,128)}, f32[2,256,1024]{2,1,0:T(8,128)}, u32[]{:S(2)}, u32[]{:S(2)}) %collective-permute-start) | collective-permute-done | bytes 2097184 | tf_op jit(solution)/shard_map/ppermute | solution.py:12
  39.0 5.1 %pad_maximum_fusion = f32[2,768,1024]{2,1,0:T(8,128)} fusion(f32[2,256,1024]{2,1,0:T(8,128)} %collective-permute-done, f32[2,512,1024]{2,1,0:T(8,128)S(1)} %copy-done), kind=kLoop, calls=%fused_computation.53 | loop fusion | flops 1572864 | bytes 12582912 | tf_op jit(solution)/shard_map/concatenate | solution.py:89
  44.2 3.4 %broadcast_in_dim.4 = f32[2,768,1024]{2,1,0:T(8,128)} broadcast(f32[]{:T(128)} %constant.22.clone.1), dimensions={} | broadcast | bytes 6291460 | tf_op jit(solution)/shard_map/broadcast_in_dim | solution.py:107
  47.6 35.1 %while.12 = (s32[]{:T(128)}, f32[2,768,1024]{2,1,0:T(8,128)}, f32[2,2,256,256]{3,2,0,1:T(8,128)S(1)}, s32[]{:T(128)}, s32[8,2]{0,1:T(2,128)S(1)}, /*index=5*/f32...) while((s32[]{:T(128)}, f32[2,768,1024]{2,1,0:T(8,128)}, ...), condition=%wide.region_4.5_spmd, body=%wide.region_0.4_spmd.sunk | while | flops 1082195968 | bytes 27525448 | solution.py:109
  52.8 1.3 dynamic-slice_bitcast_fusion.3
  55.2 1.0 fusion.67
  57.8 1.3 maximum_add_fusion.4
  59.3 4.4 %dynamic_update_slice.4 = f32[2,768,1024]{2,1,0:T(8,128)} dynamic-update-slice(f32[2,768,1024]{2,1,0:T(8,128)} %get-tuple-element.198, f32[2,256,256]{2,1,0:T(8,128)S(1)} %maximum_add_fusion.4, s32[]{:T(128)} %constant.12.clone.1..sunk, s32[]{:T(128)S(6)} %select_n.47, s32[]{:T(128)S(6)} %select_n.48) | dynamic-update-slice | bytes 1048580 | tf_op jit(solution)/shard_map/while/body/dynamic_update_slice | solution.py:81
  68.8 1.3 dynamic-slice_bitcast_fusion.3
  71.4 1.0 fusion.67
  73.9 1.4 maximum_add_fusion.4
  75.5 6.6 %dynamic_update_slice.4 = f32[2,768,1024]{2,1,0:T(8,128)} dynamic-update-slice(f32[2,768,1024]{2,1,0:T(8,128)} %get-tuple-element.198, f32[2,256,256]{2,1,0:T(8,128)S(1)} %maximum_add_fusion.4, s32[]{:T(128)} %constant.12.clone.1..sunk, s32[]{:T(128)S(6)} %select_n.47, s32[]{:T(128)S(6)} %select_n.48) | dynamic-update-slice | bytes 1048580 | tf_op jit(solution)/shard_map/while/body/dynamic_update_slice | solution.py:81
  82.8 3.2 %slice.61 = f32[2,256,1024]{2,1,0:T(8,128)} slice(f32[2,768,1024]{2,1,0:T(8,128)} %get-tuple-element.51), slice={[0:2], [512:768], [0:1024]} | slice | bytes 4194304 | tf_op jit(solution)/shard_map/slice | solution.py:112
  85.9 22.3 %collective-permute-start.1 = (f32[2,256,1024]{2,1,0:T(8,128)}, f32[2,256,1024]{2,1,0:T(8,128)}, u32[]{:S(2)}, u32[]{:S(2)}) collective-permute-start(f32[2,256,1024]{2,1,0:T(8,128)} %slice.61), channel_id=1, source_target_pairs={{0,1},{1,2},{2,3},{3,4},{4,5},{5,6},{6,7},{7,8},{8,9},{9,10},{10,1... | collective-permute-start | bytes 6291464 | tf_op jit(solution)/shard_map/ppermute | solution.py:12
  108.2 1.1 copy.11
  109.3 184.3 %all-reduce.3.cloned.1.call-done = f32[1024,256]{1,0:T(8,128)} async-done(((f32[1024,256]{1,0:T(8,128)}), f32[1024,256]{1,0:T(8,128)}) %all-reduce.3.cloned.1.call-update) | async-done | bytes 1048592 | tf_op jit(solution)/shard_map/psum | solution.py:117
  293.6 1.5 constant_dynamic-slice_fusion.1
  295.1 5.8 %pad_add_fusion = f32[2,512,1024]{2,1,0:T(8,128)} fusion(f32[2,256,1024]{2,1,0:T(8,128)} %collective-permute-done.1, f32[2,768,1024]{2,1,0:T(8,128)} %get-tuple-element.51), kind=kLoop, calls=%fused_computation.54 | loop fusion | flops 1048576 | bytes 10485760 | tf_op jit(solution)/shard_map/add | solution.py:113
  (40 shorter events, 7.4 us)
Async XLA Ops:
  7.2 5.9 %copy-start.1 = (f32[2,2,256,256]{3,2,1,0:T(8,128)S(1)}, f32[2,2,256,256]{3,2,1,0:T(8,128)}, u32[]{:S(2)}) copy-start(f32[2,2,256,256]{3,2,1,0:T(8,128)} %param.8) | copy-start | bytes 3145732
  7.2 286.5 %all-reduce.3.cloned.1.call-start = ((), (), s32[]{:S(2)}) async-start(), calls=%async_computation | async-start | bytes 2097152 | tf_op jit(solution)/shard_map/psum | solution.py:117
  10.5 28.6 %collective-permute-start = (f32[2,256,1024]{2,1,0:T(8,128)}, f32[2,256,1024]{2,1,0:T(8,128)}, u32[]{:S(2)}, u32[]{:S(2)}) collective-permute-start(f32[2,256,1024]{2,1,0:T(8,128)} %slice.59), channel_id=1, source_target_pairs={{1,0},{2,1},{3,2},{4,3},{5,4},{6,5},{7,6},{8,7},{9,8},{10,9},{11,1... | collective-permute-start | bytes 6291464 | tf_op jit(solution)/shard_map/ppermute | solution.py:12
  16.1 23.0 %copy-start = (f32[2,512,1024]{2,1,0:T(8,128)S(1)}, f32[2,512,1024]{2,1,0:T(8,128)}, u32[]{:S(2)}) copy-start(f32[2,512,1024]{2,1,0:T(8,128)} %param.7) | copy-start | bytes 12582916
  44.1 3.5 %copy-start.2 = (s32[1,8,2]{1,2,0:T(2,128)S(1)}, s32[1,8,2]{1,2,0:T(2,128)}, u32[]{:S(2)}) copy-start(s32[1,8,2]{1,2,0:T(2,128)} %param.9) | copy-start | bytes 196
  85.9 209.2 %collective-permute-start.1 = (f32[2,256,1024]{2,1,0:T(8,128)}, f32[2,256,1024]{2,1,0:T(8,128)}, u32[]{:S(2)}, u32[]{:S(2)}) collective-permute-start(f32[2,256,1024]{2,1,0:T(8,128)} %slice.61), channel_id=1, source_target_pairs={{0,1},{1,2},{2,3},{3,4},{4,5},{5,6},{6,7},{7,8},{8,9},{9,10},{10,1... | collective-permute-start | bytes 6291464 | tf_op jit(solution)/shard_map/ppermute | solution.py:12
Sparse Core Ops, SparseCore 0:
  109.4 184.1 all-reduce.2
where the time goes:
time: 314 us; the launch traced here: 308 us
  waiting for transfers between devices  202 us (64%)
  local copies, waits for them, and re-layouts  30.9 us (10%)
  starting transfers between devices  24.9 us (8%)
  other arithmetic  22.7 us (7%)
  between operations  14.1 us (4%)
  loops' own time  9.77 us (3%)
  matrix products  3.72 us (1%)
    psum x1, waiting for transfers between devices, on_device(): whole_probe = lax.psum(flat_probe, 'tr')  184 us
    ppermute x2, starting transfers between devices, shifted(): lax.ppermute(value, axis, [(source, source + steps) for source in range(i...  24.9 us
    ppermute x2, waiting for transfers between devices, shifted(): lax.ppermute(value, axis, [(source, source + steps) for source in range(i...  17.3 us
    dynamic_update_slice x2, local copies, waits for them, and re-layouts, add_block(): return lax.dynamic_update_slice(gradient, current + block, corner)  11 us
    another operation x1, loops' own time, on_device(): lax.fori_loop(jnp.int32(0), own_count, local_slot, (zero_grad, zero_probe))  9.77 us
  transfers between devices with their start and end apart: 3, of which 2 were waited for; matrix products, arithmetic and copies ran while one was open for 4% of the time, Pallas kernels for 0%

commit v1 on v0

v1 whole, which is shorter than its diff:
```python
import functools

import jax
import jax.numpy as jnp
import ml_dtypes
import numpy as np
from jax import lax
from jax.experimental import pallas as pl
from jax.experimental.pallas import tpu as pltpu
from jax.sharding import PartitionSpec as P

loss_scale = 1.0 / 1024.0
LANES = 128


def shifted(value, axis, steps):
    count = lax.axis_size(axis)
    initial, last = (max(0, -steps), min(count, count - steps))
    return lax.ppermute(value, axis, [(source, source + steps) for source in range(initial, last)])


def dft_tables(size):
    index = np.arange(size)
    angle = -2.0 * np.pi / size * (index[:, None] * index[None, :] % size)
    scale = 1.0 / np.sqrt(size)
    real = np.cos(angle) * scale
    imag = np.sin(angle) * scale
    table = np.block([[real, imag], [-imag, real]]).astype(np.float32)
    table = table.astype(ml_dtypes.bfloat16)
    return table, np.ascontiguousarray(table.T)


def one_slot(row, col, obj, acc, probe, d_ref, dt_ref, counts, probe_acc, work):
    wave, far, grad, patch = work
    size = probe.shape[-1]
    modes = probe.shape[0] // 2
    blocks = size // LANES
    chunk = 64
    first = jnp.minimum(col // LANES, obj.shape[1] - blocks - 1)
    shift = col - first * LANES
    lane = lax.broadcasted_iota(jnp.int32, (chunk, LANES), 1)
    back_by = lax.rem(LANES - shift, LANES)
    for lo in range(0, size, chunk):
        rows = pl.ds(lo, chunk)
        parts = []
        for plane in range(2):
            rolled = [
                pltpu.roll(obj[plane, first + j, pl.ds(row + lo, chunk), :], back_by, 1)
                for j in range(blocks + 1)
            ]
            part = jnp.concatenate(
                [
                    jnp.where(lane < LANES - shift, rolled[j], rolled[j + 1])
                    for j in range(blocks)
                ],
                axis=1,
            )
            patch[plane, rows, :] = part
            parts.append(part)
        o_re, o_im = parts
        for m in range(modes):
            p_re = probe[2 * m, rows, :]
            p_im = probe[2 * m + 1, rows, :]
            wave[pl.ds(m * size + lo, chunk), :size] = (p_re * o_re - p_im * o_im).astype(
                jnp.bfloat16
            )
            wave[pl.ds(m * size + lo, chunk), size:] = (p_re * o_im + p_im * o_re).astype(
                jnp.bfloat16
            )
    for part in range(2):
        half = jnp.dot(
            wave[...], d_ref[:, part * size : (part + 1) * size], preferred_element_type=jnp.float32
        ).astype(jnp.bfloat16)
        for m in range(modes):
            grad[part * size : (part + 1) * size, m * size : (m + 1) * size] = half[
                m * size : (m + 1) * size
            ]
    for m in range(modes):
        far[:, m * size : (m + 1) * size] = jnp.dot(
            dt_ref[...], grad[:, m * size : (m + 1) * size], preferred_element_type=jnp.float32
        )
    step = 16
    for lo in range(0, size, step):
        re = [far[pl.ds(lo, step), m * size : (m + 1) * size] for m in range(modes)]
        im = [far[pl.ds(size + lo, step), m * size : (m + 1) * size] for m in range(modes)]
        power = 1.0
        for m in range(modes):
            power = power + (re[m] * re[m] + im[m] * im[m])
        count = counts[pl.ds(lo, step), :].astype(jnp.float32)
        ratio = count * lax.rsqrt(jnp.maximum(count, 1.0) * power)
        factor = 2.0 * loss_scale - (2.0 * loss_scale) * ratio
        for m in range(modes):
            grad[pl.ds(lo, step), m * size : (m + 1) * size] = (re[m] * factor).astype(jnp.bfloat16)
            grad[pl.ds(size + lo, step), m * size : (m + 1) * size] = (im[m] * factor).astype(
                jnp.bfloat16
            )
    for m in range(modes):
        back = jnp.dot(
            d_ref[...], grad[:, m * size : (m + 1) * size], preferred_element_type=jnp.float32
        ).astype(jnp.bfloat16)
        for part in range(2):
            wave[m * size : (m + 1) * size, part * size : (part + 1) * size] = back[
                part * size : (part + 1) * size
            ]
    for part in range(2):
        far[:, part * size : (part + 1) * size] = jnp.dot(
            wave[...], dt_ref[:, part * size : (part + 1) * size], preferred_element_type=jnp.float32
        )
    step = 32
    lane = lax.broadcasted_iota(jnp.int32, (step, LANES), 1)
    forth_by = lax.rem(shift, LANES)
    for lo in range(0, size, step):
        rows = pl.ds(lo, step)
        sums = None
        o_re = patch[0, rows, :]
        o_im = patch[1, rows, :]
        for m in range(modes):
            g_re = far[pl.ds(m * size + lo, step), :size]
            g_im = far[pl.ds(m * size + lo, step), size:]
            p_re = probe[2 * m, rows, :]
            p_im = probe[2 * m + 1, rows, :]
            probe_acc[2 * m, rows, :] += o_re * g_re + o_im * g_im
            probe_acc[2 * m + 1, rows, :] += o_re * g_im - o_im * g_re
            term = (p_re * g_re + p_im * g_im, p_re * g_im - p_im * g_re)
            sums = term if sums is None else (sums[0] + term[0], sums[1] + term[1])
        for plane in range(2):
            rolled = [
                pltpu.roll(sums[plane][:, j * LANES : (j + 1) * LANES], forth_by, 1)
                for j in range(blocks)
            ]
            for j in range(blocks + 1):
                left = rolled[j - 1] if j > 0 else 0.0
                right = rolled[j] if j < blocks else 0.0
                acc[plane, first + j, pl.ds(row + lo, step), :] += jnp.where(
                    lane >= shift, right, left
                )


def column_copies(source, target, sem, rows_from, rows_to, count):
    out = []
    for j in range(target.shape[1] if len(target.shape) == 4 else source.shape[1]):
        if len(target.shape) == 4:
            a = source.at[:, pl.ds(rows_from, count), pl.ds(j * LANES, LANES)]
            b = target.at[:, j, pl.ds(rows_to, count), :]
        else:
            a = source.at[:, j, pl.ds(rows_from, count), :]
            b = target.at[:, pl.ds(rows_to, count), pl.ds(j * LANES, LANES)]
        out.append(pltpu.make_async_copy(a, b, sem))
    return out


def inner_kernel(
    offs, cnt, obj_hbm, probe, d_ref, dt_ref, meas_hbm, acc, probe_acc,
    obj, counts, wave, far, grad, patch, sem_obj, sem_meas,
):
    size = probe.shape[-1]
    strip = obj.shape[2]
    slots = meas_hbm.shape[1]
    copies = column_copies(obj_hbm, obj, sem_obj, 0, 0, strip)
    for c in copies:
        c.start()
    used = cnt[0]

    def is_mine(s):
        return jnp.logical_and(s < used, offs[0, s, 0] <= strip - size)

    def fetch(s):
        return pltpu.make_async_copy(meas_hbm.at[0, s], counts.at[s], sem_meas.at[s])

    for s in range(slots):
        @pl.when(is_mine(s))
        def _():
            fetch(s).start()

    acc[...] = jnp.zeros_like(acc)
    probe_acc[...] = jnp.zeros_like(probe_acc)
    for c in copies:
        c.wait()

    @pl.loop(0, used)
    def _(s):
        @pl.when(offs[0, s, 0] <= strip - size)
        def _():
            fetch(s).wait()
            one_slot(
                offs[0, s, 0], offs[0, s, 1], obj, acc, probe, d_ref, dt_ref, counts.at[s],
                probe_acc, (wave, far, grad, patch),
            )


def edge_kernel(
    offs, cnt, obj_hbm, halo, probe, d_ref, dt_ref, meas_hbm, acc_in, probe_in,
    grad_hbm, edge, probe_acc,
    obj, acc, counts, wave, far, grad, patch, sem_obj, sem_meas,
):
    size = probe.shape[-1]
    strip = obj_hbm.shape[1]
    own = strip - size
    slots = meas_hbm.shape[1]
    copies = column_copies(obj_hbm, obj, sem_obj, size, 0, own)
    for c in copies:
        c.start()
    used = cnt[0]

    def fetch(s):
        return pltpu.make_async_copy(meas_hbm.at[0, s], counts.at[s], sem_meas.at[s])

    for s in range(slots):
        @pl.when(jnp.logical_and(s < used, offs[0, s, 0] > own))
        def _():
            fetch(s).start()

    probe_acc[...] = probe_in[...]
    for j in range(obj.shape[1]):
        acc[:, j, :own, :] = acc_in[:, j, size:, :]
        acc[:, j, own:, :] = jnp.zeros((2, size, LANES), jnp.float32)
        obj[:, j, own:, :] = halo[:, :, j * LANES : (j + 1) * LANES].astype(jnp.float32)
    for c in copies:
        c.wait()

    @pl.loop(0, used)
    def _(s):
        @pl.when(offs[0, s, 0] > own)
        def _():
            fetch(s).wait()
            one_slot(
                offs[0, s, 0] - size, offs[0, s, 1], obj, acc, probe, d_ref, dt_ref, counts.at[s],
                probe_acc, (wave, far, grad, patch),
            )

    outs = column_copies(acc, grad_hbm, sem_obj, 0, size, own)
    for c in outs:
        c.start()
    for j in range(obj.shape[1]):
        edge[:, :, j * LANES : (j + 1) * LANES] = acc[:, j, own:, :].astype(jnp.bfloat16)
    for c in outs:
        c.wait()


def final_kernel(grad_in, acc, edge, grad_hbm, stage, sem):
    del grad_in
    size = edge.shape[1]
    copies = []
    for j in range(acc.shape[1]):
        stage[:, j, :, :] = acc[:, j, :size, :] + edge[:, :, j * LANES : (j + 1) * LANES].astype(
            jnp.float32
        )
        copies += [
            pltpu.make_async_copy(
                stage.at[:, j],
                grad_hbm.at[:, pl.ds(0, size), pl.ds(j * LANES, LANES)],
                sem,
            )
        ]
        copies[-1].start()
    for c in copies:
        c.wait()


def reduce_to_shares(flat, axis):
    count = lax.axis_size(axis)
    share = flat.shape[0] // count
    place = lax.axis_index(axis)
    value = flat
    bit = 1
    while bit < count:
        mine = jnp.bitwise_and(place // bit, 1)
        value = value.reshape(-1, 2, share, flat.shape[1])
        keep = lax.dynamic_index_in_dim(value, mine, 1, keepdims=False)
        send = lax.dynamic_index_in_dim(value, 1 - mine, 1, keepdims=False)
        got = lax.ppermute(
            send.astype(jnp.bfloat16), axis, [(s, s ^ bit) for s in range(count)]
        )
        value = keep + got.astype(jnp.float32)
        bit *= 2
    return value.reshape(share, flat.shape[1])


def on_device(object_field, probe_modes, scan_offsets, scan_counts, measured):
    size = probe_modes.shape[-1]
    modes = probe_modes.shape[0]
    strip, cols = object_field.shape[1:]
    slots = measured.shape[1]
    blocks = cols // LANES
    table, table_t = dft_tables(size)
    d_mat = jnp.asarray(table)
    dt_mat = jnp.asarray(table_t)
    probe = probe_modes.reshape(2 * modes, size, size)
    halo = shifted(object_field[:, :size, :].astype(jnp.bfloat16), "tr", -1)

    f32 = jnp.float32
    bf16 = jnp.bfloat16
    vmem = pl.BlockSpec(memory_space=pltpu.VMEM)
    smem = pl.BlockSpec(memory_space=pltpu.SMEM)
    hbm = pl.BlockSpec(memory_space=pl.ANY)
    work = [
        pltpu.VMEM((modes * size, 2 * size), bf16),
        pltpu.VMEM((2 * size, modes * size), f32),
        pltpu.VMEM((2 * size, modes * size), bf16),
        pltpu.VMEM((2, size, size), f32),
    ]
    sems = [pltpu.SemaphoreType.DMA, pltpu.SemaphoreType.DMA((slots,))]
    params = pltpu.CompilerParams(vmem_limit_bytes=36 * 1024 * 1024)
    cost = pl.CostEstimate(
        flops=16 * modes * size * size * size * 4 * slots // 2, bytes_accessed=8 << 20, transcendentals=0
    )
    acc, probe_acc = pl.pallas_call(
        inner_kernel,
        out_shape=(
            jax.ShapeDtypeStruct((2, blocks, strip, LANES), f32),
            jax.ShapeDtypeStruct((2 * modes, size, size), f32),
        ),
        in_specs=[smem, smem, hbm, vmem, vmem, vmem, hbm],
        out_specs=(vmem, vmem),
        scratch_shapes=[
            pltpu.VMEM((2, blocks, strip, LANES), f32),
            pltpu.VMEM((slots, size, size), jnp.int32),
        ]
        + work
        + sems,
        compiler_params=params,
        cost_estimate=cost,
        name="inner",
    )(scan_offsets, scan_counts, object_field, probe, d_mat, dt_mat, measured)
    grad, edge, probe_acc = pl.pallas_call(
        edge_kernel,
        out_shape=(
            jax.ShapeDtypeStruct(object_field.shape, f32),
            jax.ShapeDtypeStruct((2, size, cols), bf16),
            jax.ShapeDtypeStruct((2 * modes, size, size), f32),
        ),
        in_specs=[smem, smem, hbm, vmem, vmem, vmem, vmem, hbm, vmem, vmem],
        out_specs=(hbm, vmem, vmem),
        scratch_shapes=[
            pltpu.VMEM((2, blocks, strip, LANES), f32),
            pltpu.VMEM((2, blocks, strip, LANES), f32),
            pltpu.VMEM((slots, size, size), jnp.int32),
        ]
        + work
        + sems,
        compiler_params=params,
        cost_estimate=cost,
        name="edge",
    )(
        scan_offsets, scan_counts, object_field, halo, probe, d_mat, dt_mat, measured, acc, probe_acc
    )
    edge = shifted(edge, "tr", 1)
    probe_grad = reduce_to_shares(probe_acc.reshape(-1, size), "tr")
    object_grad = pl.pallas_call(
        final_kernel,
        out_shape=jax.ShapeDtypeStruct(object_field.shape, f32),
        in_specs=[hbm, vmem, vmem],
        out_specs=hbm,
        scratch_shapes=[pltpu.VMEM((2, blocks, size, LANES), f32), pltpu.SemaphoreType.DMA],
        input_output_aliases={0: 0},
        compiler_params=pltpu.CompilerParams(vmem_limit_bytes=16 * 1024 * 1024),
        name="finish",
    )(grad, acc, edge)
    return (object_grad, probe_grad)


def solution(mesh):
    return jax.shard_map(
        on_device,
        mesh=mesh,
        in_specs=(
            P(None, ("groups", "tr"), None),
            P(),
            P(("groups", "tr"), None, None),
            P(("groups", "tr")),
            P(("groups", "tr"), None, None, None),
        ),
        out_specs=(P(None, ("groups", "tr"), None), P(("groups", "tr"), None)),
        check_vma=False,
    )
```

time: 314 us -> 64 us (0.20); the launches traced: 308 us -> 64 us
  waiting for transfers between devices: 202 us -> 21.7 us
  Pallas kernels: 0 us -> 23.3 us
  other arithmetic: 22.7 us -> 0.74 us
  starting transfers between devices: 24.9 us -> 4.93 us
  local copies, waits for them, and re-layouts: 30.9 us -> 11.9 us
  between operations: 14.1 us -> 1.43 us
  loops' own time: 9.77 us -> 0 us
  matrix products: 3.72 us -> 0 us
    psum x1 -> x0, waiting for transfers between devices: 184 us -> none  [on_device(): whole_probe = lax.psum(flat_probe, 'tr')]
    pallas_call x0 -> x3, Pallas kernels: none -> 23.3 us  [the longest x1 11.5 us: on_device(): pl.pallas_call(edge_kernel, out_shape=(jax.ShapeDtypeStruct(object_field....]
    ppermute x0 -> x4, waiting for transfers between devices: none -> 21.7 us  [reduce_to_shares(): lax.ppermute(send.astype(jnp.bfloat16), axis, [(s, s ^ bit) for s in rang...]
    ppermute x2, starting transfers between devices: 24.9 us -> 4.5 us  [shifted(): lax.ppermute(value, axis, [(source, source + steps) for source in range(i...]
    ppermute x2, waiting for transfers between devices: 17.3 us -> 0.01 us  [shifted(): lax.ppermute(value, axis, [(source, source + steps) for source in range(i...]
    dynamic_update_slice x2 -> x0, local copies, waits for them, and re-layouts: 11 us -> none  [add_block(): return lax.dynamic_update_slice(gradient, current + block, corner)]
    another operation x1 -> x0, loops' own time: 9.77 us -> none  [on_device(): lax.fori_loop(jnp.int32(0), own_count, local_slot, (zero_grad, zero_probe))]
    add x5 -> x3, other arithmetic: 8.97 us -> 0.11 us  [reduce_to_shares(): value = keep + got.astype(jnp.float32)]
  transfers between devices with their start and end apart: 3 -> 6, of which waited for: 2 -> 4; matrix products, arithmetic and copies ran while one was open for 4% -> 2% of each run, Pallas kernels for 0% -> 16%
where the time goes in v1:
time: 64 us
  Pallas kernels  23.3 us (36%)
  waiting for transfers between devices  21.7 us (34%)
  local copies, waits for them, and re-layouts  11.9 us (19%)
  starting transfers between devices  4.93 us (8%)
  between operations  1.43 us (2%)
  other arithmetic  0.74 us (1%)
    ppermute x4, waiting for transfers between devices, reduce_to_shares(): lax.ppermute(send.astype(jnp.bfloat16), axis, [(s, s ^ bit) for s in rang...  21.7 us
    pallas_call x1, Pallas kernels, on_device(): pl.pallas_call(edge_kernel, out_shape=(jax.ShapeDtypeStruct(object_field....  11.5 us
    pallas_call x1, Pallas kernels, on_device(): pl.pallas_call(inner_kernel, out_shape=(jax.ShapeDtypeStruct((2, blocks,...  10.4 us
    unnamed x15, local copies, waits for them, and re-layouts  10 us
    ppermute x2, starting transfers between devices, shifted(): lax.ppermute(value, axis, [(source, source + steps) for source in range(i...  4.5 us
    slice x1, local copies, waits for them, and re-layouts, on_device(): halo = shifted(object_field[:, :size, :].astype(jnp.bfloat16), 'tr', -1)  1.75 us
    pallas_call x1, Pallas kernels, on_device(): pl.pallas_call(final_kernel, out_shape=jax.ShapeDtypeStruct(object_field....  1.35 us
  transfers between devices with their start and end apart: 6, of which 4 were waited for; matrix products, arithmetic and copies ran while one was open for 2% of the time, Pallas kernels for 16%

profile of v1, /device:TPU:13, one launch (start us, length us, event | category | flops | bytes accessed | tf_op | source)
XLA Modules:
  0.0 64.0 jit_solution(12227986063996668644)
XLA Ops:
  0.6 1.8 %slice.7 = bf16[2,256,1024]{2,1,0:T(8,128)(2,1)S(1)} slice(f32[2,512,1024]{2,1,0:T(8,128)} %obj_hbm.3), slice={[0:2], [0:256], [0:1024]} | slice | bytes 2097152 | tf_op jit(solution)/shard_map/slice | solution.py:289
  2.4 2.6 %collective-permute-start = (bf16[2,256,1024]{2,1,0:T(8,128)(2,1)S(1)}, bf16[2,256,1024]{2,1,0:T(8,128)(2,1)S(1)}, u32[]{:S(2)}, u32[]{:S(2)}) collective-permute-start(bf16[2,256,1024]{2,1,0:T(8,128)(2,1)S(1)} %slice.7), channel_id=1, source_target_pairs={{1,0},{2,1},{3,2},{4,3},{5,4},{6,5},{7,6},{8,7},{9,8},{10,9},{11,1... | collective-permute-start | bytes 3145736 | tf_op jit(solution)/shard_map/ppermute | solution.py:19
  5.6 0.8 %copy.15.offs = s32[1,8,2]{2,1,0:T(8,128)S(1)} copy(s32[1,8,2]{1,2,0:T(2,128)} %param.9) | data formatting | bytes 128 | tf_op args[2]
  6.4 2.2 %copy-done.2 = f32[2,512,1024]{2,1,0:T(8,128)S(1)} copy-done((f32[2,512,1024]{2,1,0:T(8,128)S(1)}, f32[2,512,1024]{2,1,0:T(8,128)}, u32[]{:S(2)}) %copy-start.2) | copy-done | bytes 4194328
  8.6 1.6 %copy-done.3 = s32[1,8,256,256]{3,2,1,0:T(8,128)S(1)} copy-done((s32[1,8,256,256]{3,2,1,0:T(8,128)S(1)}, s32[1,8,256,256]{3,2,1,0:T(8,128)}, u32[]{:S(2)}) %copy-start.3) | copy-done | bytes 2097176
  10.2 1.2 %copy-done.4 = f32[2,2,256,256]{3,2,1,0:T(8,128)S(1)} copy-done((f32[2,2,256,256]{3,2,1,0:T(8,128)S(1)}, f32[2,2,256,256]{3,2,1,0:T(8,128)}, u32[]{:S(2)}) %copy-start.4) | copy-done | bytes 1048600
  11.4 1.0 %copy-done.5 = bf16[512,512]{1,0:T(8,128)(2,1)S(1)} copy-done((bf16[512,512]{1,0:T(8,128)(2,1)S(1)}, bf16[512,512]{1,0:T(8,128)(2,1)}, u32[]{:S(2)}) %copy-start.5) | copy-done | bytes 524312
  12.4 1.0 %copy-done.6 = bf16[512,512]{1,0:T(8,128)(2,1)S(1)} copy-done((bf16[512,512]{1,0:T(8,128)(2,1)S(1)}, bf16[512,512]{1,0:T(8,128)(2,1)}, u32[]{:S(2)}) %copy-start.6) | copy-done | bytes 524312
  13.5 10.4 %inner.1 = (f32[2,8,512,128]{3,2,1,0:T(8,128)S(1)}, f32[4,256,256]{2,1,0:T(8,128)S(1)}) custom-call(s32[1,8,2]{2,1,0:T(8,128)S(1)} %copy.15.offs, s32[1]{0:T(128)S(6)} %copy.19.cnt, f32[2,512,1024]{2,1,0:T(8,128)S(1)} %copy-done.2, f32[4,256,256]{2,1,0:T(8,128)S(1)} %bitcast.24, bf16[512,512]{1,0:T(8,128)(2,1)S(1)} %copy-done.6, ...), custom_call_target="tpu_custom_call" | custom-call | flops 8589934592 | bytes 8388608 | tf_op jit(solution)/shard_map/inner/pallas_call | solution.py:307
  23.9 0.0 collective-permute-done.halo
  24.0 11.5 %edge.1 = (f32[2,512,1024]{2,1,0:T(8,128)}, bf16[2,256,1024]{2,1,0:T(8,128)(2,1)S(1)}, f32[4,256,256]{2,1,0:T(8,128)S(1)}) custom-call(s32[1,8,2]{2,1,0:T(8,128)S(1)} %copy.15.offs, s32[1]{0:T(128)S(6)} %copy.19.cnt, f32[2,512,1024]{2,1,0:T(8,128)S(1)} %copy-done.2, bf16[2,256,1024]{2,1,0:T(8,128)(2,1)S(1)} %collective-permute-done.halo, ...), custom_call_target="tpu_custom_call" | custom-call | flops 8589934592 | bytes 8388608 | tf_op jit(solution)/shard_map/edge/pallas_call | solution.py:325
  35.5 0.1 collective-permute-start.2
  35.6 1.5 %collective-permute-done.2 = bf16[8,64,256]{2,1,0:T(8,128)(2,1)S(1)} collective-permute-done((bf16[8,64,256]{2,1,0:T(8,128)(2,1)S(1)}, bf16[8,64,256]{2,1,0:T(8,128)(2,1)S(1)}, u32[]{:S(2)}, u32[]{:S(2)}) %collective-permute-start.2) | collective-permute-done | bytes 262176 | tf_op jit(solution)/shard_map/ppermute | solution.py:271
  37.1 0.1 bitcast_add_fusion
  37.2 0.1 collective-permute-start.3
  37.3 1.9 %collective-permute-start.1 = (bf16[2,256,1024]{2,1,0:T(8,128)(2,1)S(1)}, bf16[2,256,1024]{2,1,0:T(8,128)(2,1)S(1)}, u32[]{:S(2)}, u32[]{:S(2)}) collective-permute-start(bf16[2,256,1024]{2,1,0:T(8,128)(2,1)S(1)} %get-tuple-element.10), channel_id=1, source_target_pairs={{0,1},{1,2},{2,3},{3,4},{4,5},{5,6},{6,7},{7,8},{8,9},{9,10},{10,1... | collective-permute-start | bytes 3145736 | tf_op jit(solution)/shard_map/ppermute | solution.py:19
  39.2 3.0 %collective-permute-done.3 = bf16[4,64,256]{2,1,0:T(8,128)(2,1)S(1)} collective-permute-done((bf16[4,64,256]{2,1,0:T(8,128)(2,1)S(1)}, bf16[4,64,256]{2,1,0:T(8,128)(2,1)S(1)}, u32[]{:S(2)}, u32[]{:S(2)}) %collective-permute-start.3) | collective-permute-done | bytes 131104 | tf_op jit(solution)/shard_map/ppermute | solution.py:271
  42.2 0.2 collective-permute-start.4
  42.4 13.6 %collective-permute-done.4 = bf16[2,64,256]{2,1,0:T(8,128)(2,1)S(1)} collective-permute-done((bf16[2,64,256]{2,1,0:T(8,128)(2,1)S(1)}, bf16[2,64,256]{2,1,0:T(8,128)(2,1)S(1)}, u32[]{:S(2)}, u32[]{:S(2)}) %collective-permute-start.4) | collective-permute-done | bytes 65568 | tf_op jit(solution)/shard_map/ppermute | solution.py:271
  56.1 0.1 collective-permute-start.5
  56.2 3.7 %collective-permute-done.5 = bf16[1,64,256]{2,1,0:T(8,128)(2,1)S(1)} collective-permute-done((bf16[1,64,256]{2,1,0:T(8,128)(2,1)S(1)}, bf16[1,64,256]{2,1,0:T(8,128)(2,1)S(1)}, u32[]{:S(2)}, u32[]{:S(2)}) %collective-permute-start.5) | collective-permute-done | bytes 32800 | tf_op jit(solution)/shard_map/ppermute | solution.py:271
  59.8 0.6 add_bitcast_fusion
  60.4 2.2 %copy-done.1 = f32[2,8,512,128]{3,2,1,0:T(8,128)S(1)} copy-done((f32[2,8,512,128]{3,2,1,0:T(8,128)S(1)}, f32[2,8,512,128]{3,2,1,0:T(8,128)}, u32[]{:S(2)}) %copy-start.1) | copy-done | bytes 4194328
  62.6 1.4 %finish.1 = f32[2,512,1024]{2,1,0:T(8,128)} custom-call(f32[2,512,1024]{2,1,0:T(8,128)} %get-tuple-element.9.grad_in, f32[2,8,512,128]{3,2,1,0:T(8,128)S(1)} %copy-done.1, bf16[2,256,1024]{2,1,0:T(8,128)(2,1)S(1)} %collective-permute-done.1.edge), custom_call_target="tpu_custom_call", output_to_operand_aliasing={{}: (0, {})} | custom-call | tf_op jit(solution)/shard_map/finish/pallas_call | solution.py:349
  (15 shorter events, 0.1 us)
Async XLA Ops:
  2.4 21.6 %collective-permute-start = (bf16[2,256,1024]{2,1,0:T(8,128)(2,1)S(1)}, bf16[2,256,1024]{2,1,0:T(8,128)(2,1)S(1)}, u32[]{:S(2)}, u32[]{:S(2)}) collective-permute-start(bf16[2,256,1024]{2,1,0:T(8,128)(2,1)S(1)} %slice.7), channel_id=1, source_target_pairs={{1,0},{2,1},{3,2},{4,3},{5,4},{6,5},{7,6},{8,7},{9,8},{10,9},{11,1... | collective-permute-start | bytes 3145736 | tf_op jit(solution)/shard_map/ppermute | solution.py:19
  6.4 2.2 %copy-start.2 = (f32[2,512,1024]{2,1,0:T(8,128)S(1)}, f32[2,512,1024]{2,1,0:T(8,128)}, u32[]{:S(2)}) copy-start(f32[2,512,1024]{2,1,0:T(8,128)} %obj_hbm.3) | copy-start | bytes 12582916
  8.6 1.6 %copy-start.3 = (s32[1,8,256,256]{3,2,1,0:T(8,128)S(1)}, s32[1,8,256,256]{3,2,1,0:T(8,128)}, u32[]{:S(2)}) copy-start(s32[1,8,256,256]{3,2,1,0:T(8,128)} %meas_hbm.3) | copy-start | bytes 6291460
  10.2 1.2 %copy-start.4 = (f32[2,2,256,256]{3,2,1,0:T(8,128)S(1)}, f32[2,2,256,256]{3,2,1,0:T(8,128)}, u32[]{:S(2)}) copy-start(f32[2,2,256,256]{3,2,1,0:T(8,128)} %param.8) | copy-start | bytes 3145732
  11.4 1.0 %copy-start.5 = (bf16[512,512]{1,0:T(8,128)(2,1)S(1)}, bf16[512,512]{1,0:T(8,128)(2,1)}, u32[]{:S(2)}) copy-start(bf16[512,512]{1,0:T(8,128)(2,1)} %constant.81.clone.dt_ref) | copy-start | bytes 1572868
  12.4 1.0 %copy-start.6 = (bf16[512,512]{1,0:T(8,128)(2,1)S(1)}, bf16[512,512]{1,0:T(8,128)(2,1)}, u32[]{:S(2)}) copy-start(bf16[512,512]{1,0:T(8,128)(2,1)} %constant.80.clone.d_ref) | copy-start | bytes 1572868
  23.9 11.5 %copy-start = (f32[2,8,512,128]{3,2,1,0:T(8,128)}, f32[2,8,512,128]{3,2,1,0:T(8,128)S(1)}, u32[]{:S(2)}) copy-start(f32[2,8,512,128]{3,2,1,0:T(8,128)S(1)} %get-tuple-element.7.acc_in.acc) | copy-start | bytes 12582916
  35.5 1.6 %collective-permute-start.2 = (bf16[8,64,256]{2,1,0:T(8,128)(2,1)S(1)}, bf16[8,64,256]{2,1,0:T(8,128)(2,1)S(1)}, u32[]{:S(2)}, u32[]{:S(2)}) collective-permute-start(bf16[8,64,256]{2,1,0:T(8,128)(2,1)S(1)} %fusion), channel_id=1, source_target_pairs={{0,1},{1,0},{2,3},{3,2},{4,5},{5,4},{6,7},{7,6},{8,9},{9,8},{10,11... | collective-permute-start | bytes 786440 | tf_op jit(solution)/shard_map/ppermute | solution.py:271
  37.2 5.0 %collective-permute-start.3 = (bf16[4,64,256]{2,1,0:T(8,128)(2,1)S(1)}, bf16[4,64,256]{2,1,0:T(8,128)(2,1)S(1)}, u32[]{:S(2)}, u32[]{:S(2)}) collective-permute-start(bf16[4,64,256]{2,1,0:T(8,128)(2,1)S(1)} %fusion.1), channel_id=1, source_target_pairs={{0,2},{1,3},{2,0},{3,1},{4,6},{5,7},{6,4},{7,5},{8,10},{9,11},{10,... | collective-permute-start | bytes 393224 | tf_op jit(solution)/shard_map/ppermute | solution.py:271
  37.3 23.2 %collective-permute-start.1 = (bf16[2,256,1024]{2,1,0:T(8,128)(2,1)S(1)}, bf16[2,256,1024]{2,1,0:T(8,128)(2,1)S(1)}, u32[]{:S(2)}, u32[]{:S(2)}) collective-permute-start(bf16[2,256,1024]{2,1,0:T(8,128)(2,1)S(1)} %get-tuple-element.10), channel_id=1, source_target_pairs={{0,1},{1,2},{2,3},{3,4},{4,5},{5,6},{6,7},{7,8},{8,9},{9,10},{10,1... | collective-permute-start | bytes 3145736 | tf_op jit(solution)/shard_map/ppermute | solution.py:19
  42.2 13.8 %collective-permute-start.4 = (bf16[2,64,256]{2,1,0:T(8,128)(2,1)S(1)}, bf16[2,64,256]{2,1,0:T(8,128)(2,1)S(1)}, u32[]{:S(2)}, u32[]{:S(2)}) collective-permute-start(bf16[2,64,256]{2,1,0:T(8,128)(2,1)S(1)} %fusion.2), channel_id=1, source_target_pairs={{0,4},{1,5},{2,6},{3,7},{4,0},{5,1},{6,2},{7,3},{8,12},{9,13},{10,... | collective-permute-start | bytes 196616 | tf_op jit(solution)/shard_map/ppermute | solution.py:271
  56.1 3.7 %collective-permute-start.5 = (bf16[1,64,256]{2,1,0:T(8,128)(2,1)S(1)}, bf16[1,64,256]{2,1,0:T(8,128)(2,1)S(1)}, u32[]{:S(2)}, u32[]{:S(2)}) collective-permute-start(bf16[1,64,256]{2,1,0:T(8,128)(2,1)S(1)} %dynamic-slice_convert_fusion.2), channel_id=1, source_target_pairs={{0,8},{1,9},{2,10},{3,11},{4,12},{5,13},{6,14},{7,15},{8,0},{9,1},... | collective-permute-start | bytes 98312 | tf_op jit(solution)/shard_map/ppermute | solution.py:271
  60.4 2.2 %copy-start.1 = (f32[2,8,512,128]{3,2,1,0:T(8,128)S(1)}, f32[2,8,512,128]{3,2,1,0:T(8,128)}, u32[]{:S(2)}) copy-start(f32[2,8,512,128]{3,2,1,0:T(8,128)} %copy-done) | copy-start | bytes 12582916

commit v2 on v1

v2 whole, which is shorter than its diff:
```python
import functools

import jax
import jax.numpy as jnp
import ml_dtypes
import numpy as np
from jax import lax
from jax.experimental import pallas as pl
from jax.experimental.pallas import tpu as pltpu
from jax.sharding import PartitionSpec as P

loss_scale = 1.0 / 1024.0
LANES = 128


def shifted(value, axis, steps):
    count = lax.axis_size(axis)
    initial, last = (max(0, -steps), min(count, count - steps))
    return lax.ppermute(value, axis, [(source, source + steps) for source in range(initial, last)])


def dft_tables(size):
    index = np.arange(size)
    angle = -2.0 * np.pi / size * (index[:, None] * index[None, :] % size)
    scale = 1.0 / np.sqrt(size)
    real = np.cos(angle) * scale
    imag = np.sin(angle) * scale
    table = np.block([[real, imag], [-imag, real]]).astype(np.float32)
    table = table.astype(ml_dtypes.bfloat16)
    return table, np.ascontiguousarray(table.T)


def one_slot(row, col, obj, acc, probe, d_ref, dt_ref, counts, wait_counts, probe_acc, work):
    wave, far, grad, patch = work
    size = probe.shape[-1]
    modes = probe.shape[0] // 2
    blocks = size // LANES
    chunk = 64
    first = jnp.minimum(col // LANES, obj.shape[1] - blocks - 1)
    shift = col - first * LANES
    lane = lax.broadcasted_iota(jnp.int32, (chunk, LANES), 1)
    back_by = lax.rem(LANES - shift, LANES)
    for lo in range(0, size, chunk):
        rows = pl.ds(lo, chunk)
        parts = []
        for plane in range(2):
            rolled = [
                pltpu.roll(obj[plane, first + j, pl.ds(row + lo, chunk), :], back_by, 1)
                for j in range(blocks + 1)
            ]
            part = jnp.concatenate(
                [
                    jnp.where(lane < LANES - shift, rolled[j], rolled[j + 1])
                    for j in range(blocks)
                ],
                axis=1,
            )
            patch[plane, rows, :] = part
            parts.append(part)
        o_re, o_im = parts
        for m in range(modes):
            p_re = probe[2 * m, rows, :]
            p_im = probe[2 * m + 1, rows, :]
            wave[pl.ds(m * size + lo, chunk), :size] = (p_re * o_re - p_im * o_im).astype(
                jnp.bfloat16
            )
            wave[pl.ds(m * size + lo, chunk), size:] = (p_re * o_im + p_im * o_re).astype(
                jnp.bfloat16
            )
    for part in range(2):
        half = jnp.dot(
            wave[...], d_ref[:, part * size : (part + 1) * size], preferred_element_type=jnp.float32
        ).astype(jnp.bfloat16)
        for m in range(modes):
            grad[part * size : (part + 1) * size, m * size : (m + 1) * size] = half[
                m * size : (m + 1) * size
            ]
    for m in range(modes):
        far[:, m * size : (m + 1) * size] = jnp.dot(
            dt_ref[...], grad[:, m * size : (m + 1) * size], preferred_element_type=jnp.float32
        )
    wait_counts()
    step = 16
    for lo in range(0, size, step):
        re = [far[pl.ds(lo, step), m * size : (m + 1) * size] for m in range(modes)]
        im = [far[pl.ds(size + lo, step), m * size : (m + 1) * size] for m in range(modes)]
        power = 1.0
        for m in range(modes):
            power = power + (re[m] * re[m] + im[m] * im[m])
        count = counts[pl.ds(lo, step), :].astype(jnp.float32)
        ratio = count * lax.rsqrt(jnp.maximum(count, 1.0) * power)
        factor = 2.0 * loss_scale - (2.0 * loss_scale) * ratio
        for m in range(modes):
            grad[pl.ds(lo, step), m * size : (m + 1) * size] = (re[m] * factor).astype(jnp.bfloat16)
            grad[pl.ds(size + lo, step), m * size : (m + 1) * size] = (im[m] * factor).astype(
                jnp.bfloat16
            )
    for m in range(modes):
        back = jnp.dot(
            d_ref[...], grad[:, m * size : (m + 1) * size], preferred_element_type=jnp.float32
        ).astype(jnp.bfloat16)
        for part in range(2):
            wave[m * size : (m + 1) * size, part * size : (part + 1) * size] = back[
                part * size : (part + 1) * size
            ]
    for part in range(2):
        far[:, part * size : (part + 1) * size] = jnp.dot(
            wave[...], dt_ref[:, part * size : (part + 1) * size], preferred_element_type=jnp.float32
        )
    step = 32
    lane = lax.broadcasted_iota(jnp.int32, (step, LANES), 1)
    forth_by = lax.rem(shift, LANES)
    for lo in range(0, size, step):
        rows = pl.ds(lo, step)
        sums = None
        o_re = patch[0, rows, :]
        o_im = patch[1, rows, :]
        for m in range(modes):
            g_re = far[pl.ds(m * size + lo, step), :size]
            g_im = far[pl.ds(m * size + lo, step), size:]
            p_re = probe[2 * m, rows, :]
            p_im = probe[2 * m + 1, rows, :]
            probe_acc[2 * m, rows, :] += o_re * g_re + o_im * g_im
            probe_acc[2 * m + 1, rows, :] += o_re * g_im - o_im * g_re
            term = (p_re * g_re + p_im * g_im, p_re * g_im - p_im * g_re)
            sums = term if sums is None else (sums[0] + term[0], sums[1] + term[1])
        for plane in range(2):
            rolled = [
                pltpu.roll(sums[plane][:, j * LANES : (j + 1) * LANES], forth_by, 1)
                for j in range(blocks)
            ]
            for j in range(blocks + 1):
                left = rolled[j - 1] if j > 0 else 0.0
                right = rolled[j] if j < blocks else 0.0
                acc[plane, first + j, pl.ds(row + lo, step), :] += jnp.where(
                    lane >= shift, right, left
                )


def counts_copy(meas_hbm, counts, sem, s):
    return pltpu.make_async_copy(meas_hbm.at[0, s], counts.at[s], sem.at[s])


def inner_kernel(
    offs, cnt, obj_hbm, probe_hbm, d_hbm, dt_hbm, meas_hbm,
    obj, acc, probe_acc, probe, d_ref, dt_ref,
    counts, wave, far, grad, patch, sem_obj, sem_meas,
):
    size = probe.shape[-1]
    strip = obj_hbm.shape[1]
    slots = meas_hbm.shape[1]
    copies = [
        pltpu.make_async_copy(
            obj_hbm.at[:, :, pl.ds(j * LANES, LANES)], obj.at[:, j, pl.ds(0, strip), :], sem_obj
        )
        for j in range(obj.shape[1])
    ]
    copies += [
        pltpu.make_async_copy(probe_hbm, probe, sem_obj),
        pltpu.make_async_copy(d_hbm, d_ref, sem_obj),
        pltpu.make_async_copy(dt_hbm, dt_ref, sem_obj),
    ]
    for c in copies:
        c.start()
    used = cnt[0]

    for s in range(slots):

        @pl.when(jnp.logical_and(s < used, offs[0, s, 0] <= strip - size))
        def _():
            counts_copy(meas_hbm, counts, sem_meas, s).start()

    acc[...] = jnp.zeros_like(acc)
    probe_acc[...] = jnp.zeros_like(probe_acc)
    for c in copies:
        c.wait()

    @pl.loop(0, used)
    def _(s):
        @pl.when(offs[0, s, 0] <= strip - size)
        def _():
            one_slot(
                offs[0, s, 0], offs[0, s, 1], obj, acc, probe, d_ref, dt_ref, counts.at[s],
                counts_copy(meas_hbm, counts, sem_meas, s).wait,
                probe_acc, (wave, far, grad, patch),
            )


def edge_kernel(
    axis, offs, cnt, halo, obj_in, acc_in, probe_in, probe, d_ref, dt_ref, meas_hbm,
    obj, acc, edge_top, edge_low, keep, send, probe_acc,
    counts, wave, far, grad, patch, sem_meas,
):
    del obj_in, acc_in, probe_in
    size = probe.shape[-1]
    strip = obj.shape[2] - size
    slots = meas_hbm.shape[1]
    used = cnt[0]

    for s in range(slots):

        @pl.when(jnp.logical_and(s < used, offs[0, s, 0] > strip - size))
        def _():
            counts_copy(meas_hbm, counts, sem_meas, s).start()

    for j in range(obj.shape[1]):
        obj[:, j, strip:, :] = halo[:, :, j * LANES : (j + 1) * LANES].astype(jnp.float32)

    @pl.loop(0, used)
    def _(s):
        @pl.when(offs[0, s, 0] > strip - size)
        def _():
            one_slot(
                offs[0, s, 0], offs[0, s, 1], obj, acc, probe, d_ref, dt_ref, counts.at[s],
                counts_copy(meas_hbm, counts, sem_meas, s).wait,
                probe_acc, (wave, far, grad, patch),
            )

    half = size // 2
    for j in range(obj.shape[1]):
        cols = slice(j * LANES, (j + 1) * LANES)
        edge_top[:, :, cols] = acc[:, j, strip : strip + half, :].astype(jnp.bfloat16)
        edge_low[:, :, cols] = acc[:, j, strip + half :, :].astype(jnp.bfloat16)
    mine = lax.rem(lax.axis_index(axis), 2)
    blocks, share = keep.shape[:2]
    flat = probe_acc.reshape(2 * blocks * share, size)
    for k in range(blocks):
        keep[k] = flat[pl.ds(pl.multiple_of((2 * k + mine) * share, share), share), :]
        send[k] = flat[pl.ds(pl.multiple_of((2 * k + 1 - mine) * share, share), share), :].astype(
            jnp.bfloat16
        )


def split_kernel(axis, bit, value, got, keep, send):
    mine = lax.rem(lax.axis_index(axis) // bit, 2)
    keep[...] = value[:, mine] + got[:, mine].astype(jnp.float32)
    send[...] = (value[:, 1 - mine] + got[:, 1 - mine].astype(jnp.float32)).astype(jnp.bfloat16)


def lower_kernel(acc, grad_hbm, sem):
    strip = grad_hbm.shape[1]
    start = acc.shape[2] - strip
    copies = [
        pltpu.make_async_copy(
            acc.at[:, j, pl.ds(start, strip - start), :],
            grad_hbm.at[:, pl.ds(start, strip - start), pl.ds(j * LANES, LANES)],
            sem,
        )
        for j in range(acc.shape[1])
    ]
    for c in copies:
        c.start()
    for c in copies:
        c.wait()


def final_kernel(grad_in, acc, edge_top, edge_low, mine, other, grad_hbm, probe_grad, stage, sem):
    del grad_in
    half = edge_top.shape[1]
    copies = []
    for j in range(acc.shape[1]):
        cols = slice(j * LANES, (j + 1) * LANES)
        stage[:, j, :half, :] = acc[:, j, :half, :] + edge_top[:, :, cols].astype(jnp.float32)
        stage[:, j, half:, :] = acc[:, j, half : 2 * half, :] + edge_low[:, :, cols].astype(
            jnp.float32
        )
        copies += [
            pltpu.make_async_copy(
                stage.at[:, j],
                grad_hbm.at[:, pl.ds(0, 2 * half), pl.ds(j * LANES, LANES)],
                sem,
            )
        ]
        copies[-1].start()
    probe_grad[...] = mine[...] + other[...].astype(jnp.float32)
    for c in copies:
        c.wait()


def reduce_and_pass_edges(keep, send, edges, axis, params):
    vmem = pl.BlockSpec(memory_space=pltpu.VMEM)
    devices = lax.axis_size(axis)
    blocks, share, lanes = keep.shape
    arrived = []
    bit = 1
    while True:
        stage = bit.bit_length() - 1
        if stage in (1, 2):
            edge = edges[stage - 1]
            edge, send = lax.optimization_barrier((edge, send))
            arrived.append(shifted(edge, axis, 1))
        got = lax.ppermute(send, axis, [(s, s ^ bit) for s in range(devices)])
        bit *= 2
        if bit >= devices:
            return keep, got, arrived
        blocks //= 2
        shape = (blocks, 2, share, lanes)
        keep, send = pl.pallas_call(
            functools.partial(split_kernel, axis, bit),
            out_shape=(
                jax.ShapeDtypeStruct((blocks, share, lanes), jnp.float32),
                jax.ShapeDtypeStruct((blocks, share, lanes), jnp.bfloat16),
            ),
            in_specs=[vmem, vmem],
            out_specs=(vmem, vmem),
            compiler_params=params,
            name="split",
        )(keep.reshape(shape), got.reshape(shape))


def gradients(object_field, probe_modes, scan_offsets, scan_counts, measured):
    size = probe_modes.shape[-1]
    modes = probe_modes.shape[0]
    strip, cols = object_field.shape[1:]
    slots = measured.shape[1]
    blocks = cols // LANES
    table, table_t = dft_tables(size)
    d_mat = jnp.asarray(table)
    dt_mat = jnp.asarray(table_t)
    probe = probe_modes.reshape(2 * modes, size, size)
    halo = shifted(object_field[:, :size, :].astype(jnp.bfloat16), "tr", -1)

    f32 = jnp.float32
    bf16 = jnp.bfloat16
    vmem = pl.BlockSpec(memory_space=pltpu.VMEM)
    smem = pl.BlockSpec(memory_space=pltpu.SMEM)
    hbm = pl.BlockSpec(memory_space=pltpu.HBM)
    work = [
        pltpu.VMEM((slots, size, size), jnp.int32),
        pltpu.VMEM((modes * size, 2 * size), bf16),
        pltpu.VMEM((2 * size, modes * size), f32),
        pltpu.VMEM((2 * size, modes * size), bf16),
        pltpu.VMEM((2, size, size), f32),
    ]
    params = pltpu.CompilerParams(vmem_limit_bytes=16 * 1024 * 1024)
    cost = pl.CostEstimate(
        flops=16 * modes * size * size * size * 4 * slots // 2, bytes_accessed=8 << 20, transcendentals=0
    )
    in_hbm = lambda x: pltpu.with_memory_space_constraint(x, pltpu.HBM)
    probe, d_mat, dt_mat = in_hbm(probe), in_hbm(d_mat), in_hbm(dt_mat)
    object_hbm, measured = in_hbm(object_field), in_hbm(measured)
    tall = jax.ShapeDtypeStruct((2, blocks, strip + size, LANES), f32)
    planes = jax.ShapeDtypeStruct((2 * modes, size, size), f32)
    square = jax.ShapeDtypeStruct((2 * size, 2 * size), bf16)
    obj, acc, probe_acc, probe, d_mat, dt_mat = pl.pallas_call(
        inner_kernel,
        out_shape=(tall, tall, planes, planes, square, square),
        in_specs=[smem, smem, hbm, hbm, hbm, hbm, hbm],
        out_specs=(vmem,) * 6,
        scratch_shapes=work + [pltpu.SemaphoreType.DMA, pltpu.SemaphoreType.DMA((slots,))],
        compiler_params=params,
        cost_estimate=cost,
        name="inner",
    )(scan_offsets, scan_counts, object_hbm, probe, d_mat, dt_mat, measured)
    devices = lax.axis_size("tr")
    shares = (devices // 2, 2 * modes * size // devices, size)
    _, acc, edge_top, edge_low, keep, send, _ = pl.pallas_call(
        functools.partial(edge_kernel, "tr"),
        out_shape=(
            tall,
            tall,
            jax.ShapeDtypeStruct((2, size // 2, cols), bf16),
            jax.ShapeDtypeStruct((2, size // 2, cols), bf16),
            jax.ShapeDtypeStruct(shares, f32),
            jax.ShapeDtypeStruct(shares, bf16),
            planes,
        ),
        in_specs=[smem, smem, vmem, vmem, vmem, vmem, vmem, vmem, vmem, hbm],
        out_specs=(vmem,) * 7,
        scratch_shapes=work + [pltpu.SemaphoreType.DMA((slots,))],
        input_output_aliases={3: 0, 4: 1, 5: 6},
        compiler_params=params,
        cost_estimate=cost,
        name="edge",
    )(scan_offsets, scan_counts, halo, obj, acc, probe_acc, probe, d_mat, dt_mat, measured)
    small = pltpu.CompilerParams(vmem_limit_bytes=8 * 1024 * 1024)
    own, other, edges = reduce_and_pass_edges(keep, send, (edge_top, edge_low), "tr", small)
    grad = pl.pallas_call(
        lower_kernel,
        out_shape=jax.ShapeDtypeStruct(object_field.shape, f32),
        in_specs=[vmem],
        out_specs=hbm,
        scratch_shapes=[pltpu.SemaphoreType.DMA],
        compiler_params=small,
        name="lower",
    )(acc)
    return pl.pallas_call(
        final_kernel,
        out_shape=(
            jax.ShapeDtypeStruct(object_field.shape, f32),
            jax.ShapeDtypeStruct(own.shape[1:], f32),
        ),
        in_specs=[hbm, vmem, vmem, vmem, vmem, vmem],
        out_specs=(hbm, vmem),
        scratch_shapes=[pltpu.VMEM((2, blocks, size, LANES), f32), pltpu.SemaphoreType.DMA],
        input_output_aliases={0: 0},
        compiler_params=small,
        name="finish",
    )(grad, acc, *edges, own[0], other[0])


def solution(mesh):
    return jax.shard_map(
        gradients,
        mesh=mesh,
        in_specs=(
            P(None, ("groups", "tr"), None),
            P(),
            P(("groups", "tr"), None, None),
            P(("groups", "tr")),
            P(("groups", "tr"), None, None, None),
        ),
        out_specs=(P(None, ("groups", "tr"), None), P(("groups", "tr"), None)),
        check_vma=False,
    )
```

time: 64 us -> 55.1 us (0.86)
  the two profiles are of different devices: /device:TPU:13 before, /device:TPU:31 now
where the time goes in v2:
time: 55.1 us; the launch traced here: 54.9 us
  starting transfers between devices  26.6 us (48%)
  waiting for transfers between devices  14 us (25%)
  Pallas kernels  10.4 us (19%)
  local copies, waits for them, and re-layouts  2.5 us (5%)
  between operations  1.36 us (2%)
    ppermute x4, starting transfers between devices, reduce_and_pass_edges(): got = lax.ppermute(send, axis, [(s, s ^ bit) for s in range(devices)])  21.3 us
    ppermute x4, waiting for transfers between devices, reduce_and_pass_edges(): got = lax.ppermute(send, axis, [(s, s ^ bit) for s in range(devices)])  14 us
    pallas_call x1, Pallas kernels, gradients(): pl.pallas_call(inner_kernel, out_shape=(tall, tall, planes, planes, squar...  5.83 us
    ppermute x3, starting transfers between devices, shifted(): lax.ppermute(value, axis, [(source, source + steps) for source in range(i...  5.22 us
    pallas_call x1, Pallas kernels, gradients(): pl.pallas_call(final_kernel, out_shape=(jax.ShapeDtypeStruct(object_field...  1.99 us
    slice x1, local copies, waits for them, and re-layouts, gradients(): halo = shifted(object_field[:, :size, :].astype(jnp.bfloat16), 'tr', -1)  1.75 us
    pallas_call x1, Pallas kernels, gradients(): pl.pallas_call(lower_kernel, out_shape=jax.ShapeDtypeStruct(object_field....  1.32 us
    pallas_call x1, Pallas kernels, gradients(): pl.pallas_call(functools.partial(edge_kernel, 'tr'), out_shape=(tall, tal...  1.18 us
  transfers between devices with their start and end apart: 7, of which 4 were waited for; matrix products, arithmetic and copies ran while one was open for 1% of the time, Pallas kernels for 13%

profile of v2, /device:TPU:31, one launch (start us, length us, event | category | flops | bytes accessed | tf_op | source)
XLA Modules:
  0.0 54.9 jit_solution(613058445437094657)
XLA Ops:
  0.6 1.7 %slice.7 = bf16[2,256,1024]{2,1,0:T(8,128)(2,1)S(1)} slice(f32[2,512,1024]{2,1,0:T(8,128)} %obj_hbm.1), slice={[0:2], [0:256], [0:1024]} | slice | bytes 2097152 | tf_op jit(solution)/shard_map/slice | solution.py:321
  2.4 2.6 %collective-permute-start = (bf16[2,256,1024]{2,1,0:T(8,128)(2,1)S(1)}, bf16[2,256,1024]{2,1,0:T(8,128)(2,1)S(1)}, u32[]{:S(2)}, u32[]{:S(2)}) collective-permute-start(bf16[2,256,1024]{2,1,0:T(8,128)(2,1)S(1)} %slice.7), channel_id=1, source_target_pairs={{1,0},{2,1},{3,2},{4,3},{5,4},{6,5},{7,6},{8,7},{9,8},{10,9},{11,1... | collective-permute-start | bytes 3145736 | tf_op jit(solution)/shard_map/ppermute | solution.py:19
  5.7 0.8 %copy.14.offs = s32[1,8,2]{2,1,0:T(8,128)S(1)} copy(s32[1,8,2]{1,2,0:T(2,128)} %param.9) | data formatting | bytes 128 | tf_op args[2]
  6.4 5.8 %inner.1 = (f32[2,8,768,128]{3,2,1,0:T(8,128)S(1)}, f32[2,8,768,128]{3,2,1,0:T(8,128)S(1)}, f32[4,256,256]{2,1,0:T(8,128)S(1)}, f32[4,256,256]{2,1,0:T(8,128)S(1...) custom-call(s32[1,8,2]{2,1,0:T(8,128)S(1)} %copy.14.offs, s32[1]{0:T(128)S(6)} %copy.19.cnt, ...), custom_call_target="tpu_custom_call" | custom-call | flops 8589934592 | bytes 8388608 | tf_op jit(solution)/shard_map/inner/pallas_call | solution.py:345
  12.3 0.0 collective-permute-done.halo
  12.3 1.2 %edge.1 = (f32[2,8,768,128]{3,2,1,0:T(8,128)S(1)}, f32[2,8,768,128]{3,2,1,0:T(8,128)S(1)}, bf16[2,128,1024]{2,1,0:T(8,128)(2,1)S(1)}, bf16[2,128,1024]{2,1,0:T(8...) custom-call(s32[1,8,2]{2,1,0:T(8,128)S(1)} %copy.14.offs, ...), custom_call_target="tpu_custom_call", output_to_operand_aliasing={{0}: (3, {}), {1}: (4, {}), {6}: (5, {})} | custom-call | flops 8589934592 | bytes 8388608 | tf_op jit(solution)/shard_map/edge/pallas_call | solution.py:357
  13.5 7.3 %collective-permute-start.1 = (bf16[8,64,256]{2,1,0:T(8,128)(2,1)S(1)}, bf16[8,64,256]{2,1,0:T(8,128)(2,1)S(1)}, u32[]{:S(2)}, u32[]{:S(2)}) collective-permute-start(bf16[8,64,256]{2,1,0:T(8,128)(2,1)S(1)} %get-tuple-element.32), channel_id=1, source_target_pairs={{0,1},{1,0},{2,3},{3,2},{4,5},{5,4},{6,7},{7,6},{8,9},{9,8},{10,11... | collective-permute-start | bytes 786440 | tf_op jit(solution)/shard_map/ppermute | solution.py:292
  20.7 1.2 %collective-permute-done.1 = bf16[8,64,256]{2,1,0:T(8,128)(2,1)S(1)} collective-permute-done((bf16[8,64,256]{2,1,0:T(8,128)(2,1)S(1)}, bf16[8,64,256]{2,1,0:T(8,128)(2,1)S(1)}, u32[]{:S(2)}, u32[]{:S(2)}) %collective-permute-start.1) | collective-permute-done | bytes 262176 | tf_op jit(solution)/shard_map/ppermute | solution.py:292
  21.9 0.1 split.3
  22.0 9.9 %collective-permute-start.3 = (bf16[4,64,256]{2,1,0:T(8,128)(2,1)S(1)}, bf16[4,64,256]{2,1,0:T(8,128)(2,1)S(1)}, u32[]{:S(2)}, u32[]{:S(2)}) collective-permute-start(bf16[4,64,256]{2,1,0:T(8,128)(2,1)S(1)} %get-tuple-element.37), channel_id=1, source_target_pairs={{0,2},{1,3},{2,0},{3,1},{4,6},{5,7},{6,4},{7,5},{8,10},{9,11},{10,... | collective-permute-start | bytes 393224 | tf_op jit(solution)/shard_map/ppermute | solution.py:292
  31.8 1.3 %collective-permute-start.2 = (bf16[2,128,1024]{2,1,0:T(8,128)(2,1)S(1)}, bf16[2,128,1024]{2,1,0:T(8,128)(2,1)S(1)}, u32[]{:S(2)}, u32[]{:S(2)}) collective-permute-start(bf16[2,128,1024]{2,1,0:T(8,128)(2,1)S(1)} %get-tuple-element.34), channel_id=1, source_target_pairs={{0,1},{1,2},{2,3},{3,4},{4,5},{5,6},{6,7},{7,8},{8,9},{9,10},{10,1... | collective-permute-start | bytes 1572872 | tf_op jit(solution)/shard_map/ppermute | solution.py:19
  33.1 2.2 %collective-permute-done.3 = bf16[4,64,256]{2,1,0:T(8,128)(2,1)S(1)} collective-permute-done((bf16[4,64,256]{2,1,0:T(8,128)(2,1)S(1)}, bf16[4,64,256]{2,1,0:T(8,128)(2,1)S(1)}, u32[]{:S(2)}, u32[]{:S(2)}) %collective-permute-start.3) | collective-permute-done | bytes 131104 | tf_op jit(solution)/shard_map/ppermute | solution.py:292
  35.4 1.3 %collective-permute-start.4 = (bf16[2,128,1024]{2,1,0:T(8,128)(2,1)S(1)}, bf16[2,128,1024]{2,1,0:T(8,128)(2,1)S(1)}, u32[]{:S(2)}, u32[]{:S(2)}) collective-permute-start(bf16[2,128,1024]{2,1,0:T(8,128)(2,1)S(1)} %get-tuple-element.39), channel_id=1, source_target_pairs={{0,1},{1,2},{2,3},{3,4},{4,5},{5,6},{6,7},{7,8},{8,9},{9,10},{10,1... | collective-permute-start | bytes 1572872 | tf_op jit(solution)/shard_map/ppermute | solution.py:19
  36.7 4.2 %collective-permute-start.5 = (bf16[2,64,256]{2,1,0:T(8,128)(2,1)S(1)}, bf16[2,64,256]{2,1,0:T(8,128)(2,1)S(1)}, u32[]{:S(2)}, u32[]{:S(2)}) collective-permute-start(bf16[2,64,256]{2,1,0:T(8,128)(2,1)S(1)} %get-tuple-element.41), channel_id=1, source_target_pairs={{0,4},{1,5},{2,6},{3,7},{4,0},{5,1},{6,2},{7,3},{8,12},{9,13},{10,... | collective-permute-start | bytes 196616 | tf_op jit(solution)/shard_map/ppermute | solution.py:292
  40.8 8.3 %collective-permute-done.5 = bf16[2,64,256]{2,1,0:T(8,128)(2,1)S(1)} collective-permute-done((bf16[2,64,256]{2,1,0:T(8,128)(2,1)S(1)}, bf16[2,64,256]{2,1,0:T(8,128)(2,1)S(1)}, u32[]{:S(2)}, u32[]{:S(2)}) %collective-permute-start.5) | collective-permute-done | bytes 65568 | tf_op jit(solution)/shard_map/ppermute | solution.py:292
  49.1 0.1 collective-permute-start.6
  49.2 1.3 %lower.1.grad_in = f32[2,512,1024]{2,1,0:T(8,128)} custom-call(f32[2,8,768,128]{3,2,1,0:T(8,128)S(1)} %get-tuple-element.29.acc), custom_call_target="tpu_custom_call" | custom-call | tf_op jit(solution)/shard_map/lower/pallas_call | solution.py:378
  50.5 2.3 %collective-permute-done.6 = bf16[1,64,256]{2,1,0:T(8,128)(2,1)S(1)} collective-permute-done((bf16[1,64,256]{2,1,0:T(8,128)(2,1)S(1)}, bf16[1,64,256]{2,1,0:T(8,128)(2,1)S(1)}, u32[]{:S(2)}, u32[]{:S(2)}) %collective-permute-start.6) | collective-permute-done | bytes 32800 | tf_op jit(solution)/shard_map/ppermute | solution.py:292
  52.9 0.0 collective-permute-done.2.edge_top
  52.9 0.0 collective-permute-done.4.edge_low
  52.9 2.0 %finish.1 = (f32[2,512,1024]{2,1,0:T(8,128)}, f32[64,256]{1,0:T(8,128)}) custom-call(f32[2,512,1024]{2,1,0:T(8,128)} %lower.1.grad_in, f32[2,8,768,128]{3,2,1,0:T(8,128)S(1)} %get-tuple-element.29.acc, bf16[2,128,1024]{2,1,0:T(8,128)(2,1)S(1)} %collective-permute-done.2.edge_top, ...), custom_call_target="tpu_custom_call", output_to_operand_aliasing={{0}: (0, {})} | custom-call | tf_op jit(solution)/shard_map/finish/pallas_call | solution.py:387
  (2 shorter events, 0.0 us)
Async XLA Ops:
  2.4 9.9 %collective-permute-start = (bf16[2,256,1024]{2,1,0:T(8,128)(2,1)S(1)}, bf16[2,256,1024]{2,1,0:T(8,128)(2,1)S(1)}, u32[]{:S(2)}, u32[]{:S(2)}) collective-permute-start(bf16[2,256,1024]{2,1,0:T(8,128)(2,1)S(1)} %slice.7), channel_id=1, source_target_pairs={{1,0},{2,1},{3,2},{4,3},{5,4},{6,5},{7,6},{8,7},{9,8},{10,9},{11,1... | collective-permute-start | bytes 3145736 | tf_op jit(solution)/shard_map/ppermute | solution.py:19
  13.5 8.4 %collective-permute-start.1 = (bf16[8,64,256]{2,1,0:T(8,128)(2,1)S(1)}, bf16[8,64,256]{2,1,0:T(8,128)(2,1)S(1)}, u32[]{:S(2)}, u32[]{:S(2)}) collective-permute-start(bf16[8,64,256]{2,1,0:T(8,128)(2,1)S(1)} %get-tuple-element.32), channel_id=1, source_target_pairs={{0,1},{1,0},{2,3},{3,2},{4,5},{5,4},{6,7},{7,6},{8,9},{9,8},{10,11... | collective-permute-start | bytes 786440 | tf_op jit(solution)/shard_map/ppermute | solution.py:292
  22.0 13.4 %collective-permute-start.3 = (bf16[4,64,256]{2,1,0:T(8,128)(2,1)S(1)}, bf16[4,64,256]{2,1,0:T(8,128)(2,1)S(1)}, u32[]{:S(2)}, u32[]{:S(2)}) collective-permute-start(bf16[4,64,256]{2,1,0:T(8,128)(2,1)S(1)} %get-tuple-element.37), channel_id=1, source_target_pairs={{0,2},{1,3},{2,0},{3,1},{4,6},{5,7},{6,4},{7,5},{8,10},{9,11},{10,... | collective-permute-start | bytes 393224 | tf_op jit(solution)/shard_map/ppermute | solution.py:292
  31.8 21.0 %collective-permute-start.2 = (bf16[2,128,1024]{2,1,0:T(8,128)(2,1)S(1)}, bf16[2,128,1024]{2,1,0:T(8,128)(2,1)S(1)}, u32[]{:S(2)}, u32[]{:S(2)}) collective-permute-start(bf16[2,128,1024]{2,1,0:T(8,128)(2,1)S(1)} %get-tuple-element.34), channel_id=1, source_target_pairs={{0,1},{1,2},{2,3},{3,4},{4,5},{5,6},{6,7},{7,8},{8,9},{9,10},{10,1... | collective-permute-start | bytes 1572872 | tf_op jit(solution)/shard_map/ppermute | solution.py:19
  35.4 17.5 %collective-permute-start.4 = (bf16[2,128,1024]{2,1,0:T(8,128)(2,1)S(1)}, bf16[2,128,1024]{2,1,0:T(8,128)(2,1)S(1)}, u32[]{:S(2)}, u32[]{:S(2)}) collective-permute-start(bf16[2,128,1024]{2,1,0:T(8,128)(2,1)S(1)} %get-tuple-element.39), channel_id=1, source_target_pairs={{0,1},{1,2},{2,3},{3,4},{4,5},{5,6},{6,7},{7,8},{8,9},{9,10},{10,1... | collective-permute-start | bytes 1572872 | tf_op jit(solution)/shard_map/ppermute | solution.py:19
  36.7 12.4 %collective-permute-start.5 = (bf16[2,64,256]{2,1,0:T(8,128)(2,1)S(1)}, bf16[2,64,256]{2,1,0:T(8,128)(2,1)S(1)}, u32[]{:S(2)}, u32[]{:S(2)}) collective-permute-start(bf16[2,64,256]{2,1,0:T(8,128)(2,1)S(1)} %get-tuple-element.41), channel_id=1, source_target_pairs={{0,4},{1,5},{2,6},{3,7},{4,0},{5,1},{6,2},{7,3},{8,12},{9,13},{10,... | collective-permute-start | bytes 196616 | tf_op jit(solution)/shard_map/ppermute | solution.py:292
  49.1 3.7 %collective-permute-start.6 = (bf16[1,64,256]{2,1,0:T(8,128)(2,1)S(1)}, bf16[1,64,256]{2,1,0:T(8,128)(2,1)S(1)}, u32[]{:S(2)}, u32[]{:S(2)}) collective-permute-start(bf16[1,64,256]{2,1,0:T(8,128)(2,1)S(1)} %get-tuple-element.43), channel_id=1, source_target_pairs={{0,8},{1,9},{2,10},{3,11},{4,12},{5,13},{6,14},{7,15},{8,0},{9,1},... | collective-permute-start | bytes 98312 | tf_op jit(solution)/shard_map/ppermute | solution.py:292

commit v3 on v2

--- a/solution.py
+++ b/solution.py
@@ -31,7 +31,7 @@
 
 
 def one_slot(row, col, obj, acc, probe, d_ref, dt_ref, counts, wait_counts, probe_acc, work):
-    wave, far, grad, patch = work
+    wave, far, grad, patch, probe_low = work
     size = probe.shape[-1]
     modes = probe.shape[0] // 2
     blocks = size // LANES
@@ -55,7 +55,7 @@
                 ],
                 axis=1,
             )
-            patch[plane, rows, :] = part
+            patch[plane, rows, :] = part.astype(jnp.bfloat16)
             parts.append(part)
         o_re, o_im = parts
         for m in range(modes):
@@ -104,9 +104,9 @@
                 part * size : (part + 1) * size
             ]
     for part in range(2):
-        far[:, part * size : (part + 1) * size] = jnp.dot(
+        grad[:, part * size : (part + 1) * size] = jnp.dot(
             wave[...], dt_ref[:, part * size : (part + 1) * size], preferred_element_type=jnp.float32
-        )
+        ).astype(jnp.bfloat16)
     step = 32
     lane = lax.broadcasted_iota(jnp.int32, (step, LANES), 1)
     forth_by = lax.rem(shift, LANES)
@@ -116,17 +116,19 @@
         o_re = patch[0, rows, :]
         o_im = patch[1, rows, :]
         for m in range(modes):
-            g_re = far[pl.ds(m * size + lo, step), :size]
-            g_im = far[pl.ds(m * size + lo, step), size:]
-            p_re = probe[2 * m, rows, :]
-            p_im = probe[2 * m + 1, rows, :]
-            probe_acc[2 * m, rows, :] += o_re * g_re + o_im * g_im
-            probe_acc[2 * m + 1, rows, :] += o_re * g_im - o_im * g_re
+            g_re = grad[pl.ds(m * size + lo, step), :size]
+            g_im = grad[pl.ds(m * size + lo, step), size:]
+            p_re = probe_low[2 * m, rows, :]
+            p_im = probe_low[2 * m + 1, rows, :]
+            probe_acc[2 * m, rows, :] += (o_re * g_re + o_im * g_im).astype(jnp.float32)
+            probe_acc[2 * m + 1, rows, :] += (o_re * g_im - o_im * g_re).astype(jnp.float32)
             term = (p_re * g_re + p_im * g_im, p_re * g_im - p_im * g_re)
             sums = term if sums is None else (sums[0] + term[0], sums[1] + term[1])
         for plane in range(2):
             rolled = [
-                pltpu.roll(sums[plane][:, j * LANES : (j + 1) * LANES], forth_by, 1)
+                pltpu.roll(
+                sums[plane][:, j * LANES : (j + 1) * LANES].astype(jnp.float32), forth_by, 1
+            )
                 for j in range(blocks)
             ]
             for j in range(blocks + 1):
@@ -144,7 +146,7 @@
 def inner_kernel(
     offs, cnt, obj_hbm, probe_hbm, d_hbm, dt_hbm, meas_hbm,
     obj, acc, probe_acc, probe, d_ref, dt_ref,
-    counts, wave, far, grad, patch, sem_obj, sem_meas,
+    counts, wave, far, grad, patch, probe_low, sem_obj, sem_meas,
 ):
     size = probe.shape[-1]
     strip = obj_hbm.shape[1]
@@ -166,7 +168,7 @@
 
     for s in range(slots):
 
-        @pl.when(jnp.logical_and(s < used, offs[0, s, 0] <= strip - size))
+        @pl.when(jnp.logical_and(s < used, offs[0, 0, s] <= strip - size))
         def _():
             counts_copy(meas_hbm, counts, sem_meas, s).start()
 
@@ -174,22 +176,23 @@
     probe_acc[...] = jnp.zeros_like(probe_acc)
     for c in copies:
         c.wait()
+    probe_low[...] = probe[...].astype(jnp.bfloat16)
 
     @pl.loop(0, used)
     def _(s):
-        @pl.when(offs[0, s, 0] <= strip - size)
+        @pl.when(offs[0, 0, s] <= strip - size)
         def _():
             one_slot(
-                offs[0, s, 0], offs[0, s, 1], obj, acc, probe, d_ref, dt_ref, counts.at[s],
+                offs[0, 0, s], offs[0, 1, s], obj, acc, probe, d_ref, dt_ref, counts.at[s],
                 counts_copy(meas_hbm, counts, sem_meas, s).wait,
-                probe_acc, (wave, far, grad, patch),
+                probe_acc, (wave, far, grad, patch, probe_low),
             )
 
 
 def edge_kernel(
     axis, offs, cnt, halo, obj_in, acc_in, probe_in, probe, d_ref, dt_ref, meas_hbm,
     obj, acc, edge_top, edge_low, keep, send, probe_acc,
-    counts, wave, far, grad, patch, sem_meas,
+    counts, wave, far, grad, patch, probe_low, sem_meas,
 ):
     del obj_in, acc_in, probe_in
     size = probe.shape[-1]
@@ -199,21 +202,22 @@
 
     for s in range(slots):
 
-        @pl.when(jnp.logical_and(s < used, offs[0, s, 0] > strip - size))
+        @pl.when(jnp.logical_and(s < used, offs[0, 0, s] > strip - size))
         def _():
             counts_copy(meas_hbm, counts, sem_meas, s).start()
 
+    probe_low[...] = probe[...].astype(jnp.bfloat16)
     for j in range(obj.shape[1]):
         obj[:, j, strip:, :] = halo[:, :, j * LANES : (j + 1) * LANES].astype(jnp.float32)
 
     @pl.loop(0, used)
     def _(s):
-        @pl.when(offs[0, s, 0] > strip - size)
+        @pl.when(offs[0, 0, s] > strip - size)
         def _():
             one_slot(
-                offs[0, s, 0], offs[0, s, 1], obj, acc, probe, d_ref, dt_ref, counts.at[s],
+                offs[0, 0, s], offs[0, 1, s], obj, acc, probe, d_ref, dt_ref, counts.at[s],
                 counts_copy(meas_hbm, counts, sem_meas, s).wait,
-                probe_acc, (wave, far, grad, patch),
+                probe_acc, (wave, far, grad, patch, probe_low),
             )
 
     half = size // 2
@@ -254,24 +258,31 @@
         c.wait()
 
 
-def final_kernel(grad_in, acc, edge_top, edge_low, mine, other, grad_hbm, probe_grad, stage, sem):
-    del grad_in
-    half = edge_top.shape[1]
+def add_edge(at, acc, edge, grad_hbm, stage, sem):
+    rows = edge.shape[1]
     copies = []
     for j in range(acc.shape[1]):
-        cols = slice(j * LANES, (j + 1) * LANES)
-        stage[:, j, :half, :] = acc[:, j, :half, :] + edge_top[:, :, cols].astype(jnp.float32)
-        stage[:, j, half:, :] = acc[:, j, half : 2 * half, :] + edge_low[:, :, cols].astype(
-            jnp.float32
-        )
+        stage[:, j, :, :] = acc[:, j, at : at + rows, :] + edge[
+            :, :, j * LANES : (j + 1) * LANES
+        ].astype(jnp.float32)
         copies += [
             pltpu.make_async_copy(
-                stage.at[:, j],
-                grad_hbm.at[:, pl.ds(0, 2 * half), pl.ds(j * LANES, LANES)],
-                sem,
+                stage.at[:, j], grad_hbm.at[:, pl.ds(at, rows), pl.ds(j * LANES, LANES)], sem
             )
         ]
         copies[-1].start()
+    return copies
+
+
+def top_kernel(grad_in, acc, edge, grad_hbm, stage, sem):
+    del grad_in
+    for c in add_edge(0, acc, edge, grad_hbm, stage, sem):
+        c.wait()
+
+
+def final_kernel(grad_in, acc, edge, mine, other, grad_hbm, probe_grad, stage, sem):
+    del grad_in
+    copies = add_edge(edge.shape[1], acc, edge, grad_hbm, stage, sem)
     probe_grad[...] = mine[...] + other[...].astype(jnp.float32)
     for c in copies:
         c.wait()
@@ -314,6 +325,7 @@
     strip, cols = object_field.shape[1:]
     slots = measured.shape[1]
     blocks = cols // LANES
+    scan_offsets = jnp.swapaxes(scan_offsets, 1, 2)
     table, table_t = dft_tables(size)
     d_mat = jnp.asarray(table)
     dt_mat = jnp.asarray(table_t)
@@ -330,7 +342,8 @@
         pltpu.VMEM((modes * size, 2 * size), bf16),
         pltpu.VMEM((2 * size, modes * size), f32),
         pltpu.VMEM((2 * size, modes * size), bf16),
-        pltpu.VMEM((2, size, size), f32),
+        pltpu.VMEM((2, size, size), bf16),
+        pltpu.VMEM((2 * modes, size, size), bf16),
     ]
     params = pltpu.CompilerParams(vmem_limit_bytes=16 * 1024 * 1024)
     cost = pl.CostEstimate(
@@ -384,19 +397,30 @@
         compiler_params=small,
         name="lower",
     )(acc)
+    scratch = [pltpu.VMEM((2, blocks, size // 2, LANES), f32), pltpu.SemaphoreType.DMA]
+    grad = pl.pallas_call(
+        top_kernel,
+        out_shape=jax.ShapeDtypeStruct(object_field.shape, f32),
+        in_specs=[hbm, vmem, vmem],
+        out_specs=hbm,
+        scratch_shapes=scratch,
+        input_output_aliases={0: 0},
+        compiler_params=small,
+        name="top",
+    )(grad, acc, edges[0])
     return pl.pallas_call(
         final_kernel,
         out_shape=(
             jax.ShapeDtypeStruct(object_field.shape, f32),
             jax.ShapeDtypeStruct(own.shape[1:], f32),
         ),
-        in_specs=[hbm, vmem, vmem, vmem, vmem, vmem],
+        in_specs=[hbm, vmem, vmem, vmem, vmem],
         out_specs=(hbm, vmem),
-        scratch_shapes=[pltpu.VMEM((2, blocks, size, LANES), f32), pltpu.SemaphoreType.DMA],
+        scratch_shapes=scratch,
         input_output_aliases={0: 0},
         compiler_params=small,
         name="finish",
-    )(grad, acc, *edges, own[0], other[0])
+    )(grad, acc, edges[1], own[0], other[0])
 
 
 def solution(mesh):

time: 55.1 us -> 54.5 us (0.989)
  the two profiles are of different devices: /device:TPU:31 before, /device:TPU:15 now
where the time goes in v3:
time: 54.5 us; the launch traced here: 54.2 us
  starting transfers between devices  23.3 us (43%)
  waiting for transfers between devices  16.2 us (30%)
  Pallas kernels  10.9 us (20%)
  local copies, waits for them, and re-layouts  2.42 us (4%)
  between operations  1.41 us (3%)
    ppermute x3, starting transfers between devices, shifted(): lax.ppermute(value, axis, [(source, source + steps) for source in range(i...  17.6 us
    ppermute x4, waiting for transfers between devices, reduce_and_pass_edges(): got = lax.ppermute(send, axis, [(s, s ^ bit) for s in range(devices)])  8.76 us
    ppermute x3, waiting for transfers between devices, shifted(): lax.ppermute(value, axis, [(source, source + steps) for source in range(i...  7.41 us
    ppermute x4, starting transfers between devices, reduce_and_pass_edges(): got = lax.ppermute(send, axis, [(s, s ^ bit) for s in range(devices)])  5.73 us
    pallas_call x1, Pallas kernels, gradients(): pl.pallas_call(inner_kernel, out_shape=(tall, tall, planes, planes, squar...  5.68 us
    slice x1, local copies, waits for them, and re-layouts, gradients(): halo = shifted(object_field[:, :size, :].astype(jnp.bfloat16), 'tr', -1)  1.75 us
    pallas_call x1, Pallas kernels, gradients(): pl.pallas_call(final_kernel, out_shape=(jax.ShapeDtypeStruct(object_field...  1.62 us
    pallas_call x1, Pallas kernels, gradients(): pl.pallas_call(lower_kernel, out_shape=jax.ShapeDtypeStruct(object_field....  1.31 us
  transfers between devices with their start and end apart: 7, of which 3 were waited for; matrix products, arithmetic and copies ran while one was open for 0% of the time, Pallas kernels for 15%

profile of v3, /device:TPU:15, one launch (start us, length us, event | category | flops | bytes accessed | tf_op | source)
XLA Modules:
  0.0 54.2 jit_solution(60711959084186452)
XLA Ops:
  0.6 1.7 %slice.7 = bf16[2,256,1024]{2,1,0:T(8,128)(2,1)S(1)} slice(f32[2,512,1024]{2,1,0:T(8,128)} %obj_hbm.1), slice={[0:2], [0:256], [0:1024]} | slice | bytes 2097152 | tf_op jit(solution)/shard_map/slice | solution.py:333
  2.4 2.6 %collective-permute-start = (bf16[2,256,1024]{2,1,0:T(8,128)(2,1)S(1)}, bf16[2,256,1024]{2,1,0:T(8,128)(2,1)S(1)}, u32[]{:S(2)}, u32[]{:S(2)}) collective-permute-start(bf16[2,256,1024]{2,1,0:T(8,128)(2,1)S(1)} %slice.7), channel_id=1, source_target_pairs={{1,0},{2,1},{3,2},{4,3},{5,4},{6,5},{7,6},{8,7},{9,8},{10,9},{11,1... | collective-permute-start | bytes 3145736 | tf_op jit(solution)/shard_map/ppermute | solution.py:19
  5.6 0.0 copy-start
  5.6 0.7 %copy-done = s32[1,8,2]{1,2,0:T(2,128)S(1)} copy-done((s32[1,8,2]{1,2,0:T(2,128)S(1)}, s32[1,8,2]{1,2,0:T(2,128)}, u32[]{:S(2)}) %copy-start) | copy-done | bytes 88
  6.3 5.7 %inner.1 = (f32[2,8,768,128]{3,2,1,0:T(8,128)S(1)}, f32[2,8,768,128]{3,2,1,0:T(8,128)S(1)}, f32[4,256,256]{2,1,0:T(8,128)S(1)}, f32[4,256,256]{2,1,0:T(8,128)S(1...) custom-call(s32[1,2,8]{2,1,0:T(2,128)S(1)} %bitcast.18, s32[1]{0:T(128)S(6)} %copy.19.cnt, ...), custom_call_target="tpu_custom_call" | custom-call | flops 8589934592 | bytes 8388608 | tf_op jit(solution)/shard_map/inner/pallas_call | solution.py:358
  12.0 7.4 %collective-permute-done.halo = bf16[2,256,1024]{2,1,0:T(8,128)(2,1)S(1)} collective-permute-done((bf16[2,256,1024]{2,1,0:T(8,128)(2,1)S(1)}, bf16[2,256,1024]{2,1,0:T(8,128)(2,1)S(1)}, u32[]{:S(2)}, u32[]{:S(2)}) %collective-permute-start) | collective-permute-done | bytes 1048608 | tf_op jit(solution)/shard_map/ppermute | solution.py:19
  19.4 1.2 %edge.1 = (f32[2,8,768,128]{3,2,1,0:T(8,128)S(1)}, f32[2,8,768,128]{3,2,1,0:T(8,128)S(1)}, bf16[2,128,1024]{2,1,0:T(8,128)(2,1)S(1)}, bf16[2,128,1024]{2,1,0:T(8...) custom-call(s32[1,2,8]{2,1,0:T(2,128)S(1)} %bitcast.19, ...), custom_call_target="tpu_custom_call", output_to_operand_aliasing={{0}: (3, {}), {1}: (4, {}), {6}: (5, {})} | custom-call | flops 8589934592 | bytes 8388608 | tf_op jit(solution)/shard_map/edge/pallas_call | solution.py:370
  20.6 0.1 collective-permute-start.1
  20.7 1.5 %collective-permute-done.1 = bf16[8,64,256]{2,1,0:T(8,128)(2,1)S(1)} collective-permute-done((bf16[8,64,256]{2,1,0:T(8,128)(2,1)S(1)}, bf16[8,64,256]{2,1,0:T(8,128)(2,1)S(1)}, u32[]{:S(2)}, u32[]{:S(2)}) %collective-permute-start.1) | collective-permute-done | bytes 262176 | tf_op jit(solution)/shard_map/ppermute | solution.py:303
  22.2 0.1 split.3
  22.2 1.5 %collective-permute-start.3 = (bf16[4,64,256]{2,1,0:T(8,128)(2,1)S(1)}, bf16[4,64,256]{2,1,0:T(8,128)(2,1)S(1)}, u32[]{:S(2)}, u32[]{:S(2)}) collective-permute-start(bf16[4,64,256]{2,1,0:T(8,128)(2,1)S(1)} %get-tuple-element.37), channel_id=1, source_target_pairs={{0,2},{1,3},{2,0},{3,1},{4,6},{5,7},{6,4},{7,5},{8,10},{9,11},{10,... | collective-permute-start | bytes 393224 | tf_op jit(solution)/shard_map/ppermute | solution.py:303
  23.8 9.3 %collective-permute-start.2 = (bf16[2,128,1024]{2,1,0:T(8,128)(2,1)S(1)}, bf16[2,128,1024]{2,1,0:T(8,128)(2,1)S(1)}, u32[]{:S(2)}, u32[]{:S(2)}) collective-permute-start(bf16[2,128,1024]{2,1,0:T(8,128)(2,1)S(1)} %get-tuple-element.34), channel_id=1, source_target_pairs={{0,1},{1,2},{2,3},{3,4},{4,5},{5,6},{6,7},{7,8},{8,9},{9,10},{10,1... | collective-permute-start | bytes 1572872 | tf_op jit(solution)/shard_map/ppermute | solution.py:19
  33.1 0.0 collective-permute-done.3
  33.1 0.1 split.4
  33.2 5.7 %collective-permute-start.4 = (bf16[2,128,1024]{2,1,0:T(8,128)(2,1)S(1)}, bf16[2,128,1024]{2,1,0:T(8,128)(2,1)S(1)}, u32[]{:S(2)}, u32[]{:S(2)}) collective-permute-start(bf16[2,128,1024]{2,1,0:T(8,128)(2,1)S(1)} %get-tuple-element.39), channel_id=1, source_target_pairs={{0,1},{1,2},{2,3},{3,4},{4,5},{5,6},{6,7},{7,8},{8,9},{9,10},{10,1... | collective-permute-start | bytes 1572872 | tf_op jit(solution)/shard_map/ppermute | solution.py:19
  38.9 0.1 collective-permute-start.5
  39.0 7.2 %collective-permute-done.5 = bf16[2,64,256]{2,1,0:T(8,128)(2,1)S(1)} collective-permute-done((bf16[2,64,256]{2,1,0:T(8,128)(2,1)S(1)}, bf16[2,64,256]{2,1,0:T(8,128)(2,1)S(1)}, u32[]{:S(2)}, u32[]{:S(2)}) %collective-permute-start.5) | collective-permute-done | bytes 65568 | tf_op jit(solution)/shard_map/ppermute | solution.py:303
  46.2 4.0 %collective-permute-start.6 = (bf16[1,64,256]{2,1,0:T(8,128)(2,1)S(1)}, bf16[1,64,256]{2,1,0:T(8,128)(2,1)S(1)}, u32[]{:S(2)}, u32[]{:S(2)}) collective-permute-start(bf16[1,64,256]{2,1,0:T(8,128)(2,1)S(1)} %get-tuple-element.43), channel_id=1, source_target_pairs={{0,8},{1,9},{2,10},{3,11},{4,12},{5,13},{6,14},{7,15},{8,0},{9,1},... | collective-permute-start | bytes 98312 | tf_op jit(solution)/shard_map/ppermute | solution.py:303
  50.3 1.3 %lower.1.grad_in = f32[2,512,1024]{2,1,0:T(8,128)} custom-call(f32[2,8,768,128]{3,2,1,0:T(8,128)S(1)} %get-tuple-element.29.acc), custom_call_target="tpu_custom_call" | custom-call | tf_op jit(solution)/shard_map/lower/pallas_call | solution.py:391
  51.6 0.0 collective-permute-done.2.edge
  51.6 1.0 %top.1.grad_in = f32[2,512,1024]{2,1,0:T(8,128)} custom-call(f32[2,512,1024]{2,1,0:T(8,128)} %lower.1.grad_in, f32[2,8,768,128]{3,2,1,0:T(8,128)S(1)} %get-tuple-element.29.acc, bf16[2,128,1024]{2,1,0:T(8,128)(2,1)S(1)} %collective-permute-done.2.edge), custom_call_target="tpu_custom_call", output_to_operand_aliasing={{}: (0, {})} | custom-call | tf_op jit(solution)/shard_map/top/pallas_call | solution.py:401
  52.6 0.0 collective-permute-done.6
  52.6 0.0 collective-permute-done.4.edge
  52.6 1.6 %finish.1 = (f32[2,512,1024]{2,1,0:T(8,128)}, f32[64,256]{1,0:T(8,128)}) custom-call(f32[2,512,1024]{2,1,0:T(8,128)} %top.1.grad_in, f32[2,8,768,128]{3,2,1,0:T(8,128)S(1)} %get-tuple-element.29.acc, bf16[2,128,1024]{2,1,0:T(8,128)(2,1)S(1)} %collective-permute-done.4.edge, f32[64,256]{1,0:T(8,128)S(1)} %bitcast.15, ...), custom_call_target="tpu_custom_call", output_to_operand_aliasing={{0}: (0, {})} | custom-call | tf_op jit(solution)/shard_map/finish/pallas_call | solution.py:411
  (1 shorter events, 0.0 us)
Async XLA Ops:
  2.4 17.0 %collective-permute-start = (bf16[2,256,1024]{2,1,0:T(8,128)(2,1)S(1)}, bf16[2,256,1024]{2,1,0:T(8,128)(2,1)S(1)}, u32[]{:S(2)}, u32[]{:S(2)}) collective-permute-start(bf16[2,256,1024]{2,1,0:T(8,128)(2,1)S(1)} %slice.7), channel_id=1, source_target_pairs={{1,0},{2,1},{3,2},{4,3},{5,4},{6,5},{7,6},{8,7},{9,8},{10,9},{11,1... | collective-permute-start | bytes 3145736 | tf_op jit(solution)/shard_map/ppermute | solution.py:19
  5.6 0.7 %copy-start = (s32[1,8,2]{1,2,0:T(2,128)S(1)}, s32[1,8,2]{1,2,0:T(2,128)}, u32[]{:S(2)}) copy-start(s32[1,8,2]{1,2,0:T(2,128)} %param.9) | copy-start | bytes 196
  20.6 1.6 %collective-permute-start.1 = (bf16[8,64,256]{2,1,0:T(8,128)(2,1)S(1)}, bf16[8,64,256]{2,1,0:T(8,128)(2,1)S(1)}, u32[]{:S(2)}, u32[]{:S(2)}) collective-permute-start(bf16[8,64,256]{2,1,0:T(8,128)(2,1)S(1)} %get-tuple-element.32), channel_id=1, source_target_pairs={{0,1},{1,0},{2,3},{3,2},{4,5},{5,4},{6,7},{7,6},{8,9},{9,8},{10,11... | collective-permute-start | bytes 786440 | tf_op jit(solution)/shard_map/ppermute | solution.py:303
  22.2 10.9 %collective-permute-start.3 = (bf16[4,64,256]{2,1,0:T(8,128)(2,1)S(1)}, bf16[4,64,256]{2,1,0:T(8,128)(2,1)S(1)}, u32[]{:S(2)}, u32[]{:S(2)}) collective-permute-start(bf16[4,64,256]{2,1,0:T(8,128)(2,1)S(1)} %get-tuple-element.37), channel_id=1, source_target_pairs={{0,2},{1,3},{2,0},{3,1},{4,6},{5,7},{6,4},{7,5},{8,10},{9,11},{10,... | collective-permute-start | bytes 393224 | tf_op jit(solution)/shard_map/ppermute | solution.py:303
  23.8 27.8 %collective-permute-start.2 = (bf16[2,128,1024]{2,1,0:T(8,128)(2,1)S(1)}, bf16[2,128,1024]{2,1,0:T(8,128)(2,1)S(1)}, u32[]{:S(2)}, u32[]{:S(2)}) collective-permute-start(bf16[2,128,1024]{2,1,0:T(8,128)(2,1)S(1)} %get-tuple-element.34), channel_id=1, source_target_pairs={{0,1},{1,2},{2,3},{3,4},{4,5},{5,6},{6,7},{7,8},{8,9},{9,10},{10,1... | collective-permute-start | bytes 1572872 | tf_op jit(solution)/shard_map/ppermute | solution.py:19
  33.2 19.4 %collective-permute-start.4 = (bf16[2,128,1024]{2,1,0:T(8,128)(2,1)S(1)}, bf16[2,128,1024]{2,1,0:T(8,128)(2,1)S(1)}, u32[]{:S(2)}, u32[]{:S(2)}) collective-permute-start(bf16[2,128,1024]{2,1,0:T(8,128)(2,1)S(1)} %get-tuple-element.39), channel_id=1, source_target_pairs={{0,1},{1,2},{2,3},{3,4},{4,5},{5,6},{6,7},{7,8},{8,9},{9,10},{10,1... | collective-permute-start | bytes 1572872 | tf_op jit(solution)/shard_map/ppermute | solution.py:19
  38.9 7.3 %collective-permute-start.5 = (bf16[2,64,256]{2,1,0:T(8,128)(2,1)S(1)}, bf16[2,64,256]{2,1,0:T(8,128)(2,1)S(1)}, u32[]{:S(2)}, u32[]{:S(2)}) collective-permute-start(bf16[2,64,256]{2,1,0:T(8,128)(2,1)S(1)} %get-tuple-element.41), channel_id=1, source_target_pairs={{0,4},{1,5},{2,6},{3,7},{4,0},{5,1},{6,2},{7,3},{8,12},{9,13},{10,... | collective-permute-start | bytes 196616 | tf_op jit(solution)/shard_map/ppermute | solution.py:303
  46.2 6.4 %collective-permute-start.6 = (bf16[1,64,256]{2,1,0:T(8,128)(2,1)S(1)}, bf16[1,64,256]{2,1,0:T(8,128)(2,1)S(1)}, u32[]{:S(2)}, u32[]{:S(2)}) collective-permute-start(bf16[1,64,256]{2,1,0:T(8,128)(2,1)S(1)} %get-tuple-element.43), channel_id=1, source_target_pairs={{0,8},{1,9},{2,10},{3,11},{4,12},{5,13},{6,14},{7,15},{8,0},{9,1},... | collective-permute-start | bytes 98312 | tf_op jit(solution)/shard_map/ppermute | solution.py:303

commit v4 on v3

--- a/solution.py
+++ b/solution.py
@@ -145,8 +145,8 @@
 
 def inner_kernel(
     offs, cnt, obj_hbm, probe_hbm, d_hbm, dt_hbm, meas_hbm,
-    obj, acc, probe_acc, probe, d_ref, dt_ref,
-    counts, wave, far, grad, patch, probe_low, sem_obj, sem_meas,
+    obj, acc, probe_acc, probe, d_ref, dt_ref, probe_low,
+    counts, wave, far, grad, patch, sem_obj, sem_meas,
 ):
     size = probe.shape[-1]
     strip = obj_hbm.shape[1]
@@ -190,9 +190,9 @@
 
 
 def edge_kernel(
-    axis, offs, cnt, halo, obj_in, acc_in, probe_in, probe, d_ref, dt_ref, meas_hbm,
+    axis, offs, cnt, halo, obj_in, acc_in, probe_in, probe, probe_low, d_ref, dt_ref, meas_hbm,
     obj, acc, edge_top, edge_low, keep, send, probe_acc,
-    counts, wave, far, grad, patch, probe_low, sem_meas,
+    counts, wave, far, grad, patch, sem_meas,
 ):
     del obj_in, acc_in, probe_in
     size = probe.shape[-1]
@@ -206,7 +206,6 @@
         def _():
             counts_copy(meas_hbm, counts, sem_meas, s).start()
 
-    probe_low[...] = probe[...].astype(jnp.bfloat16)
     for j in range(obj.shape[1]):
         obj[:, j, strip:, :] = halo[:, :, j * LANES : (j + 1) * LANES].astype(jnp.float32)
 
@@ -280,12 +279,14 @@
         c.wait()
 
 
-def final_kernel(grad_in, acc, edge, mine, other, grad_hbm, probe_grad, stage, sem):
+def final_kernel(grad_in, acc, edge, mine, other, grad_hbm, probe_hbm, stage, total, sem, sem_probe):
     del grad_in
-    copies = add_edge(edge.shape[1], acc, edge, grad_hbm, stage, sem)
-    probe_grad[...] = mine[...] + other[...].astype(jnp.float32)
-    for c in copies:
+    total[...] = mine[...] + other[...].astype(jnp.float32)
+    whole = pltpu.make_async_copy(total, probe_hbm, sem_probe)
+    whole.start()
+    for c in add_edge(edge.shape[1], acc, edge, grad_hbm, stage, sem):
         c.wait()
+    whole.wait()
 
 
 def reduce_and_pass_edges(keep, send, edges, axis, params):
@@ -343,7 +344,6 @@
         pltpu.VMEM((2 * size, modes * size), f32),
         pltpu.VMEM((2 * size, modes * size), bf16),
         pltpu.VMEM((2, size, size), bf16),
-        pltpu.VMEM((2 * modes, size, size), bf16),
     ]
     params = pltpu.CompilerParams(vmem_limit_bytes=16 * 1024 * 1024)
     cost = pl.CostEstimate(
@@ -354,12 +354,13 @@
     object_hbm, measured = in_hbm(object_field), in_hbm(measured)
     tall = jax.ShapeDtypeStruct((2, blocks, strip + size, LANES), f32)
     planes = jax.ShapeDtypeStruct((2 * modes, size, size), f32)
+    low_planes = jax.ShapeDtypeStruct(planes.shape, bf16)
     square = jax.ShapeDtypeStruct((2 * size, 2 * size), bf16)
-    obj, acc, probe_acc, probe, d_mat, dt_mat = pl.pallas_call(
+    obj, acc, probe_acc, probe, d_mat, dt_mat, probe_low = pl.pallas_call(
         inner_kernel,
-        out_shape=(tall, tall, planes, planes, square, square),
+        out_shape=(tall, tall, planes, planes, square, square, low_planes),
         in_specs=[smem, smem, hbm, hbm, hbm, hbm, hbm],
-        out_specs=(vmem,) * 6,
+        out_specs=(vmem,) * 7,
         scratch_shapes=work + [pltpu.SemaphoreType.DMA, pltpu.SemaphoreType.DMA((slots,))],
         compiler_params=params,
         cost_estimate=cost,
@@ -378,14 +379,14 @@
             jax.ShapeDtypeStruct(shares, bf16),
             planes,
         ),
-        in_specs=[smem, smem, vmem, vmem, vmem, vmem, vmem, vmem, vmem, hbm],
+        in_specs=[smem, smem] + [vmem] * 8 + [hbm],
         out_specs=(vmem,) * 7,
         scratch_shapes=work + [pltpu.SemaphoreType.DMA((slots,))],
         input_output_aliases={3: 0, 4: 1, 5: 6},
         compiler_params=params,
         cost_estimate=cost,
         name="edge",
-    )(scan_offsets, scan_counts, halo, obj, acc, probe_acc, probe, d_mat, dt_mat, measured)
+    )(scan_offsets, scan_counts, halo, obj, acc, probe_acc, probe, probe_low, d_mat, dt_mat, measured)
     small = pltpu.CompilerParams(vmem_limit_bytes=8 * 1024 * 1024)
     own, other, edges = reduce_and_pass_edges(keep, send, (edge_top, edge_low), "tr", small)
     grad = pl.pallas_call(
@@ -415,8 +416,9 @@
             jax.ShapeDtypeStruct(own.shape[1:], f32),
         ),
         in_specs=[hbm, vmem, vmem, vmem, vmem],
-        out_specs=(hbm, vmem),
-        scratch_shapes=scratch,
+        out_specs=(hbm, hbm),
+        scratch_shapes=scratch[:1]
+        + [pltpu.VMEM(own.shape[1:], f32), scratch[1], pltpu.SemaphoreType.DMA],
         input_output_aliases={0: 0},
         compiler_params=small,
         name="finish",

time: 54.5 us -> 53.9 us (0.989)
  Pallas kernels: 10.9 us -> 10.3 us
    pallas_call x1, Pallas kernels: 1.62 us -> 1.01 us  [gradients(): pl.pallas_call(final_kernel, out_shape=(jax.ShapeDtypeStruct(object_field...]
where the time goes in v4:
time: 53.9 us; the launch traced here: 53.7 us
  starting transfers between devices  23.4 us (43%)
  waiting for transfers between devices  16.2 us (30%)
  Pallas kernels  10.3 us (19%)
  local copies, waits for them, and re-layouts  2.42 us (4%)
  between operations  1.41 us (3%)
    ppermute x3, starting transfers between devices, shifted(): lax.ppermute(value, axis, [(source, source + steps) for source in range(i...  17.6 us
    ppermute x4, waiting for transfers between devices, reduce_and_pass_edges(): got = lax.ppermute(send, axis, [(s, s ^ bit) for s in range(devices)])  8.85 us
    ppermute x3, waiting for transfers between devices, shifted(): lax.ppermute(value, axis, [(source, source + steps) for source in range(i...  7.4 us
    ppermute x4, starting transfers between devices, reduce_and_pass_edges(): got = lax.ppermute(send, axis, [(s, s ^ bit) for s in range(devices)])  5.75 us
    pallas_call x1, Pallas kernels, gradients(): pl.pallas_call(inner_kernel, out_shape=(tall, tall, planes, planes, squar...  5.7 us
    slice x1, local copies, waits for them, and re-layouts, gradients(): halo = shifted(object_field[:, :size, :].astype(jnp.bfloat16), 'tr', -1)  1.75 us
    pallas_call x1, Pallas kernels, gradients(): pl.pallas_call(lower_kernel, out_shape=jax.ShapeDtypeStruct(object_field....  1.31 us
    pallas_call x1, Pallas kernels, gradients(): pl.pallas_call(functools.partial(edge_kernel, 'tr'), out_shape=(tall, tal...  1.13 us
  transfers between devices with their start and end apart: 7, of which 3 were waited for; matrix products, arithmetic and copies ran while one was open for 0% of the time, Pallas kernels for 15%

profile of v4, /device:TPU:15, one launch (start us, length us, event | category | flops | bytes accessed | tf_op | source)
XLA Modules:
  0.0 53.7 jit_solution(6302518991015303087)
XLA Ops:
  0.6 1.7 %slice.7 = bf16[2,256,1024]{2,1,0:T(8,128)(2,1)S(1)} slice(f32[2,512,1024]{2,1,0:T(8,128)} %obj_hbm.1), slice={[0:2], [0:256], [0:1024]} | slice | bytes 2097152 | tf_op jit(solution)/shard_map/slice | solution.py:334
  2.4 2.6 %collective-permute-start = (bf16[2,256,1024]{2,1,0:T(8,128)(2,1)S(1)}, bf16[2,256,1024]{2,1,0:T(8,128)(2,1)S(1)}, u32[]{:S(2)}, u32[]{:S(2)}) collective-permute-start(bf16[2,256,1024]{2,1,0:T(8,128)(2,1)S(1)} %slice.7), channel_id=1, source_target_pairs={{1,0},{2,1},{3,2},{4,3},{5,4},{6,5},{7,6},{8,7},{9,8},{10,9},{11,1... | collective-permute-start | bytes 3145736 | tf_op jit(solution)/shard_map/ppermute | solution.py:19
  5.6 0.0 copy-start
  5.6 0.7 %copy-done = s32[1,8,2]{1,2,0:T(2,128)S(1)} copy-done((s32[1,8,2]{1,2,0:T(2,128)S(1)}, s32[1,8,2]{1,2,0:T(2,128)}, u32[]{:S(2)}) %copy-start) | copy-done | bytes 88
  6.3 5.7 %inner.1 = (f32[2,8,768,128]{3,2,1,0:T(8,128)S(1)}, f32[2,8,768,128]{3,2,1,0:T(8,128)S(1)}, f32[4,256,256]{2,1,0:T(8,128)S(1)}, f32[4,256,256]{2,1,0:T(8,128)S(1...) custom-call(s32[1,2,8]{2,1,0:T(2,128)S(1)} %bitcast.18, ...), custom_call_target="tpu_custom_call" | custom-call | flops 8589934592 | bytes 8388608 | tf_op jit(solution)/shard_map/inner/pallas_call | solution.py:359
  12.0 7.4 %collective-permute-done.halo = bf16[2,256,1024]{2,1,0:T(8,128)(2,1)S(1)} collective-permute-done((bf16[2,256,1024]{2,1,0:T(8,128)(2,1)S(1)}, bf16[2,256,1024]{2,1,0:T(8,128)(2,1)S(1)}, u32[]{:S(2)}, u32[]{:S(2)}) %collective-permute-start) | collective-permute-done | bytes 1048608 | tf_op jit(solution)/shard_map/ppermute | solution.py:19
  19.4 1.1 %edge.1 = (f32[2,8,768,128]{3,2,1,0:T(8,128)S(1)}, f32[2,8,768,128]{3,2,1,0:T(8,128)S(1)}, bf16[2,128,1024]{2,1,0:T(8,128)(2,1)S(1)}, bf16[2,128,1024]{2,1,0:T(8...) custom-call(s32[1,2,8]{2,1,0:T(2,128)S(1)} %bitcast.19, ...), custom_call_target="tpu_custom_call", output_to_operand_aliasing={{0}: (3, {}), {1}: (4, {}), {6}: (5, {})} | custom-call | flops 8589934592 | bytes 8388608 | tf_op jit(solution)/shard_map/edge/pallas_call | solution.py:371
  20.5 0.1 collective-permute-start.1
  20.6 1.5 %collective-permute-done.1 = bf16[8,64,256]{2,1,0:T(8,128)(2,1)S(1)} collective-permute-done((bf16[8,64,256]{2,1,0:T(8,128)(2,1)S(1)}, bf16[8,64,256]{2,1,0:T(8,128)(2,1)S(1)}, u32[]{:S(2)}, u32[]{:S(2)}) %collective-permute-start.1) | collective-permute-done | bytes 262176 | tf_op jit(solution)/shard_map/ppermute | solution.py:304
  22.1 0.1 split.3
  22.2 1.6 %collective-permute-start.3 = (bf16[4,64,256]{2,1,0:T(8,128)(2,1)S(1)}, bf16[4,64,256]{2,1,0:T(8,128)(2,1)S(1)}, u32[]{:S(2)}, u32[]{:S(2)}) collective-permute-start(bf16[4,64,256]{2,1,0:T(8,128)(2,1)S(1)} %get-tuple-element.39), channel_id=1, source_target_pairs={{0,2},{1,3},{2,0},{3,1},{4,6},{5,7},{6,4},{7,5},{8,10},{9,11},{10,... | collective-permute-start | bytes 393224 | tf_op jit(solution)/shard_map/ppermute | solution.py:304
  23.8 9.3 %collective-permute-start.2 = (bf16[2,128,1024]{2,1,0:T(8,128)(2,1)S(1)}, bf16[2,128,1024]{2,1,0:T(8,128)(2,1)S(1)}, u32[]{:S(2)}, u32[]{:S(2)}) collective-permute-start(bf16[2,128,1024]{2,1,0:T(8,128)(2,1)S(1)} %get-tuple-element.36), channel_id=1, source_target_pairs={{0,1},{1,2},{2,3},{3,4},{4,5},{5,6},{6,7},{7,8},{8,9},{9,10},{10,1... | collective-permute-start | bytes 1572872 | tf_op jit(solution)/shard_map/ppermute | solution.py:19
  33.1 0.0 collective-permute-done.3
  33.1 0.1 split.4
  33.2 5.7 %collective-permute-start.4 = (bf16[2,128,1024]{2,1,0:T(8,128)(2,1)S(1)}, bf16[2,128,1024]{2,1,0:T(8,128)(2,1)S(1)}, u32[]{:S(2)}, u32[]{:S(2)}) collective-permute-start(bf16[2,128,1024]{2,1,0:T(8,128)(2,1)S(1)} %get-tuple-element.41), channel_id=1, source_target_pairs={{0,1},{1,2},{2,3},{3,4},{4,5},{5,6},{6,7},{7,8},{8,9},{9,10},{10,1... | collective-permute-start | bytes 1572872 | tf_op jit(solution)/shard_map/ppermute | solution.py:19
  38.9 0.1 collective-permute-start.5
  39.0 7.3 %collective-permute-done.5 = bf16[2,64,256]{2,1,0:T(8,128)(2,1)S(1)} collective-permute-done((bf16[2,64,256]{2,1,0:T(8,128)(2,1)S(1)}, bf16[2,64,256]{2,1,0:T(8,128)(2,1)S(1)}, u32[]{:S(2)}, u32[]{:S(2)}) %collective-permute-start.5) | collective-permute-done | bytes 65568 | tf_op jit(solution)/shard_map/ppermute | solution.py:304
  46.3 4.0 %collective-permute-start.6 = (bf16[1,64,256]{2,1,0:T(8,128)(2,1)S(1)}, bf16[1,64,256]{2,1,0:T(8,128)(2,1)S(1)}, u32[]{:S(2)}, u32[]{:S(2)}) collective-permute-start(bf16[1,64,256]{2,1,0:T(8,128)(2,1)S(1)} %get-tuple-element.45), channel_id=1, source_target_pairs={{0,8},{1,9},{2,10},{3,11},{4,12},{5,13},{6,14},{7,15},{8,0},{9,1},... | collective-permute-start | bytes 98312 | tf_op jit(solution)/shard_map/ppermute | solution.py:304
  50.4 1.3 %lower.1.grad_in = f32[2,512,1024]{2,1,0:T(8,128)} custom-call(f32[2,8,768,128]{3,2,1,0:T(8,128)S(1)} %get-tuple-element.31.acc), custom_call_target="tpu_custom_call" | custom-call | tf_op jit(solution)/shard_map/lower/pallas_call | solution.py:392
  51.7 0.0 collective-permute-done.2.edge
  51.7 1.0 %top.1.grad_in = f32[2,512,1024]{2,1,0:T(8,128)} custom-call(f32[2,512,1024]{2,1,0:T(8,128)} %lower.1.grad_in, f32[2,8,768,128]{3,2,1,0:T(8,128)S(1)} %get-tuple-element.31.acc, bf16[2,128,1024]{2,1,0:T(8,128)(2,1)S(1)} %collective-permute-done.2.edge), custom_call_target="tpu_custom_call", output_to_operand_aliasing={{}: (0, {})} | custom-call | tf_op jit(solution)/shard_map/top/pallas_call | solution.py:402
  52.7 0.0 collective-permute-done.6
  52.7 0.0 collective-permute-done.4.edge
  52.7 1.0 %finish.1 = (f32[2,512,1024]{2,1,0:T(8,128)}, f32[64,256]{1,0:T(8,128)}) custom-call(f32[2,512,1024]{2,1,0:T(8,128)} %top.1.grad_in, f32[2,8,768,128]{3,2,1,0:T(8,128)S(1)} %get-tuple-element.31.acc, bf16[2,128,1024]{2,1,0:T(8,128)(2,1)S(1)} %collective-permute-done.4.edge, f32[64,256]{1,0:T(8,128)S(1)} %bitcast.15, ...), custom_call_target="tpu_custom_call", output_to_operand_aliasing={{0}: (0, {})} | custom-call | tf_op jit(solution)/shard_map/finish/pallas_call | solution.py:412
  (1 shorter events, 0.0 us)
Async XLA Ops:
  2.4 17.0 %collective-permute-start = (bf16[2,256,1024]{2,1,0:T(8,128)(2,1)S(1)}, bf16[2,256,1024]{2,1,0:T(8,128)(2,1)S(1)}, u32[]{:S(2)}, u32[]{:S(2)}) collective-permute-start(bf16[2,256,1024]{2,1,0:T(8,128)(2,1)S(1)} %slice.7), channel_id=1, source_target_pairs={{1,0},{2,1},{3,2},{4,3},{5,4},{6,5},{7,6},{8,7},{9,8},{10,9},{11,1... | collective-permute-start | bytes 3145736 | tf_op jit(solution)/shard_map/ppermute | solution.py:19
  5.6 0.7 %copy-start = (s32[1,8,2]{1,2,0:T(2,128)S(1)}, s32[1,8,2]{1,2,0:T(2,128)}, u32[]{:S(2)}) copy-start(s32[1,8,2]{1,2,0:T(2,128)} %param.9) | copy-start | bytes 196
  20.5 1.6 %collective-permute-start.1 = (bf16[8,64,256]{2,1,0:T(8,128)(2,1)S(1)}, bf16[8,64,256]{2,1,0:T(8,128)(2,1)S(1)}, u32[]{:S(2)}, u32[]{:S(2)}) collective-permute-start(bf16[8,64,256]{2,1,0:T(8,128)(2,1)S(1)} %get-tuple-element.34), channel_id=1, source_target_pairs={{0,1},{1,0},{2,3},{3,2},{4,5},{5,4},{6,7},{7,6},{8,9},{9,8},{10,11... | collective-permute-start | bytes 786440 | tf_op jit(solution)/shard_map/ppermute | solution.py:304
  22.2 10.9 %collective-permute-start.3 = (bf16[4,64,256]{2,1,0:T(8,128)(2,1)S(1)}, bf16[4,64,256]{2,1,0:T(8,128)(2,1)S(1)}, u32[]{:S(2)}, u32[]{:S(2)}) collective-permute-start(bf16[4,64,256]{2,1,0:T(8,128)(2,1)S(1)} %get-tuple-element.39), channel_id=1, source_target_pairs={{0,2},{1,3},{2,0},{3,1},{4,6},{5,7},{6,4},{7,5},{8,10},{9,11},{10,... | collective-permute-start | bytes 393224 | tf_op jit(solution)/shard_map/ppermute | solution.py:304
  23.8 27.9 %collective-permute-start.2 = (bf16[2,128,1024]{2,1,0:T(8,128)(2,1)S(1)}, bf16[2,128,1024]{2,1,0:T(8,128)(2,1)S(1)}, u32[]{:S(2)}, u32[]{:S(2)}) collective-permute-start(bf16[2,128,1024]{2,1,0:T(8,128)(2,1)S(1)} %get-tuple-element.36), channel_id=1, source_target_pairs={{0,1},{1,2},{2,3},{3,4},{4,5},{5,6},{6,7},{7,8},{8,9},{9,10},{10,1... | collective-permute-start | bytes 1572872 | tf_op jit(solution)/shard_map/ppermute | solution.py:19
  33.2 19.5 %collective-permute-start.4 = (bf16[2,128,1024]{2,1,0:T(8,128)(2,1)S(1)}, bf16[2,128,1024]{2,1,0:T(8,128)(2,1)S(1)}, u32[]{:S(2)}, u32[]{:S(2)}) collective-permute-start(bf16[2,128,1024]{2,1,0:T(8,128)(2,1)S(1)} %get-tuple-element.41), channel_id=1, source_target_pairs={{0,1},{1,2},{2,3},{3,4},{4,5},{5,6},{6,7},{7,8},{8,9},{9,10},{10,1... | collective-permute-start | bytes 1572872 | tf_op jit(solution)/shard_map/ppermute | solution.py:19
  38.9 7.4 %collective-permute-start.5 = (bf16[2,64,256]{2,1,0:T(8,128)(2,1)S(1)}, bf16[2,64,256]{2,1,0:T(8,128)(2,1)S(1)}, u32[]{:S(2)}, u32[]{:S(2)}) collective-permute-start(bf16[2,64,256]{2,1,0:T(8,128)(2,1)S(1)} %get-tuple-element.43), channel_id=1, source_target_pairs={{0,4},{1,5},{2,6},{3,7},{4,0},{5,1},{6,2},{7,3},{8,12},{9,13},{10,... | collective-permute-start | bytes 196616 | tf_op jit(solution)/shard_map/ppermute | solution.py:304
  46.3 6.4 %collective-permute-start.6 = (bf16[1,64,256]{2,1,0:T(8,128)(2,1)S(1)}, bf16[1,64,256]{2,1,0:T(8,128)(2,1)S(1)}, u32[]{:S(2)}, u32[]{:S(2)}) collective-permute-start(bf16[1,64,256]{2,1,0:T(8,128)(2,1)S(1)} %get-tuple-element.45), channel_id=1, source_target_pairs={{0,8},{1,9},{2,10},{3,11},{4,12},{5,13},{6,14},{7,15},{8,0},{9,1},... | collective-permute-start | bytes 98312 | tf_op jit(solution)/shard_map/ppermute | solution.py:304

commit v5 on v4

--- a/solution.py
+++ b/solution.py
@@ -191,7 +191,7 @@
 
 def edge_kernel(
     axis, offs, cnt, halo, obj_in, acc_in, probe_in, probe, probe_low, d_ref, dt_ref, meas_hbm,
-    obj, acc, edge_top, edge_low, keep, send, probe_acc,
+    obj, acc, keep, send, probe_acc,
     counts, wave, far, grad, patch, sem_meas,
 ):
     del obj_in, acc_in, probe_in
@@ -219,11 +219,6 @@
                 probe_acc, (wave, far, grad, patch, probe_low),
             )
 
-    half = size // 2
-    for j in range(obj.shape[1]):
-        cols = slice(j * LANES, (j + 1) * LANES)
-        edge_top[:, :, cols] = acc[:, j, strip : strip + half, :].astype(jnp.bfloat16)
-        edge_low[:, :, cols] = acc[:, j, strip + half :, :].astype(jnp.bfloat16)
     mine = lax.rem(lax.axis_index(axis), 2)
     blocks, share = keep.shape[:2]
     flat = probe_acc.reshape(2 * blocks * share, size)
@@ -232,6 +227,15 @@
         send[k] = flat[pl.ds(pl.multiple_of((2 * k + 1 - mine) * share, share), share), :].astype(
             jnp.bfloat16
         )
+
+
+def round_kernel(acc, edge_top, edge_low):
+    half = edge_top.shape[1]
+    start = acc.shape[2] - 2 * half
+    for j in range(acc.shape[1]):
+        cols = slice(j * LANES, (j + 1) * LANES)
+        edge_top[:, :, cols] = acc[:, j, start : start + half, :].astype(jnp.bfloat16)
+        edge_low[:, :, cols] = acc[:, j, start + half :, :].astype(jnp.bfloat16)
 
 
 def split_kernel(axis, bit, value, got, keep, send):
@@ -368,26 +372,33 @@
     )(scan_offsets, scan_counts, object_hbm, probe, d_mat, dt_mat, measured)
     devices = lax.axis_size("tr")
     shares = (devices // 2, 2 * modes * size // devices, size)
-    _, acc, edge_top, edge_low, keep, send, _ = pl.pallas_call(
+    _, acc, keep, send, _ = pl.pallas_call(
         functools.partial(edge_kernel, "tr"),
         out_shape=(
             tall,
             tall,
-            jax.ShapeDtypeStruct((2, size // 2, cols), bf16),
-            jax.ShapeDtypeStruct((2, size // 2, cols), bf16),
             jax.ShapeDtypeStruct(shares, f32),
             jax.ShapeDtypeStruct(shares, bf16),
             planes,
         ),
         in_specs=[smem, smem] + [vmem] * 8 + [hbm],
-        out_specs=(vmem,) * 7,
+        out_specs=(vmem,) * 5,
         scratch_shapes=work + [pltpu.SemaphoreType.DMA((slots,))],
-        input_output_aliases={3: 0, 4: 1, 5: 6},
+        input_output_aliases={3: 0, 4: 1, 5: 4},
         compiler_params=params,
         cost_estimate=cost,
         name="edge",
     )(scan_offsets, scan_counts, halo, obj, acc, probe_acc, probe, probe_low, d_mat, dt_mat, measured)
     small = pltpu.CompilerParams(vmem_limit_bytes=8 * 1024 * 1024)
+    edge_top, edge_low = pl.pallas_call(
+        round_kernel,
+        out_shape=(jax.ShapeDtypeStruct((2, size // 2, cols), bf16),) * 2,
+        in_specs=[vmem],
+        out_specs=(vmem,) * 2,
+        compiler_params=small,
+        cost_estimate=pl.CostEstimate(flops=1 << 19, bytes_accessed=3 << 20, transcendentals=0),
+        name="rounding",
+    )(acc)
     own, other, edges = reduce_and_pass_edges(keep, send, (edge_top, edge_low), "tr", small)
     grad = pl.pallas_call(
         lower_kernel,

time: 53.9 us -> 53.7 us (level)
  transfers between devices with their start and end apart: 7 -> 7, of which waited for: 3 -> 3; matrix products, arithmetic and copies ran while one was open for 0% -> 0% of each run, Pallas kernels for 15% -> 16%
where the time goes in v5:
time: 53.7 us; the launch traced here: 53.4 us
  starting transfers between devices  23.4 us (44%)
  waiting for transfers between devices  16 us (30%)
  Pallas kernels  10.3 us (19%)
  local copies, waits for them, and re-layouts  2.42 us (5%)
  between operations  1.42 us (3%)
    ppermute x3, starting transfers between devices, shifted(): lax.ppermute(value, axis, [(source, source + steps) for source in range(i...  17.6 us
    ppermute x4, waiting for transfers between devices, reduce_and_pass_edges(): got = lax.ppermute(send, axis, [(s, s ^ bit) for s in range(devices)])  8.58 us
    ppermute x3, waiting for transfers between devices, shifted(): lax.ppermute(value, axis, [(source, source + steps) for source in range(i...  7.4 us
    ppermute x4, starting transfers between devices, reduce_and_pass_edges(): got = lax.ppermute(send, axis, [(s, s ^ bit) for s in range(devices)])  5.74 us
    pallas_call x1, Pallas kernels, gradients(): pl.pallas_call(inner_kernel, out_shape=(tall, tall, planes, planes, squar...  5.7 us
    slice x1, local copies, waits for them, and re-layouts, gradients(): halo = shifted(object_field[:, :size, :].astype(jnp.bfloat16), 'tr', -1)  1.75 us
    pallas_call x1, Pallas kernels, gradients(): pl.pallas_call(lower_kernel, out_shape=jax.ShapeDtypeStruct(object_field....  1.31 us
  transfers between devices with their start and end apart: 7, of which 3 were waited for; matrix products, arithmetic and copies ran while one was open for 0% of the time, Pallas kernels for 16%

profile of v5, /device:TPU:15, one launch (start us, length us, event | category | flops | bytes accessed | tf_op | source)
XLA Modules:
  0.0 53.4 jit_solution(17731563635359282183)
XLA Ops:
  0.6 1.7 %slice.7 = bf16[2,256,1024]{2,1,0:T(8,128)(2,1)S(1)} slice(f32[2,512,1024]{2,1,0:T(8,128)} %obj_hbm.1), slice={[0:2], [0:256], [0:1024]} | slice | bytes 2097152 | tf_op jit(solution)/shard_map/slice | solution.py:338
  2.4 2.6 %collective-permute-start = (bf16[2,256,1024]{2,1,0:T(8,128)(2,1)S(1)}, bf16[2,256,1024]{2,1,0:T(8,128)(2,1)S(1)}, u32[]{:S(2)}, u32[]{:S(2)}) collective-permute-start(bf16[2,256,1024]{2,1,0:T(8,128)(2,1)S(1)} %slice.7), channel_id=1, source_target_pairs={{1,0},{2,1},{3,2},{4,3},{5,4},{6,5},{7,6},{8,7},{9,8},{10,9},{11,1... | collective-permute-start | bytes 3145736 | tf_op jit(solution)/shard_map/ppermute | solution.py:19
  5.6 0.0 copy-start
  5.6 0.7 %copy-done = s32[1,8,2]{1,2,0:T(2,128)S(1)} copy-done((s32[1,8,2]{1,2,0:T(2,128)S(1)}, s32[1,8,2]{1,2,0:T(2,128)}, u32[]{:S(2)}) %copy-start) | copy-done | bytes 88
  6.3 5.7 %inner.1 = (f32[2,8,768,128]{3,2,1,0:T(8,128)S(1)}, f32[2,8,768,128]{3,2,1,0:T(8,128)S(1)}, f32[4,256,256]{2,1,0:T(8,128)S(1)}, f32[4,256,256]{2,1,0:T(8,128)S(1...) custom-call(s32[1,2,8]{2,1,0:T(2,128)S(1)} %bitcast.18, ...), custom_call_target="tpu_custom_call" | custom-call | flops 8589934592 | bytes 8388608 | tf_op jit(solution)/shard_map/inner/pallas_call | solution.py:363
  12.0 7.4 %collective-permute-done.halo = bf16[2,256,1024]{2,1,0:T(8,128)(2,1)S(1)} collective-permute-done((bf16[2,256,1024]{2,1,0:T(8,128)(2,1)S(1)}, bf16[2,256,1024]{2,1,0:T(8,128)(2,1)S(1)}, u32[]{:S(2)}, u32[]{:S(2)}) %collective-permute-start) | collective-permute-done | bytes 1048608 | tf_op jit(solution)/shard_map/ppermute | solution.py:19
  19.4 0.9 %edge.1 = (f32[2,8,768,128]{3,2,1,0:T(8,128)S(1)}, f32[2,8,768,128]{3,2,1,0:T(8,128)S(1)}, f32[8,64,256]{2,1,0:T(8,128)S(1)}, bf16[8,64,256]{2,1,0:T(8,128)(2,1)S(1)}, f32[4,256,256]{2,1,0:T(8,128)S(1)}) custom-call(s32[1,2,8]{2,1,0:T(2,128)S(1)} %bitcast.19, s32[1]{0:T(128)S(6)} %copy.19.cnt, ...), custom_call_target="tpu_custom_call", output_to_operand_aliasing={{0}: (3, {}), {1}: (4, {}), {4}: (5, {})} | custom-call | flops 8589934592 | bytes 8388608 | tf_op jit(solution)/shard_map/edge/pallas_call | solution.py:375
  20.3 0.1 collective-permute-start.1
  20.3 0.3 rounding.1
  20.6 1.2 %collective-permute-done.1 = bf16[8,64,256]{2,1,0:T(8,128)(2,1)S(1)} collective-permute-done((bf16[8,64,256]{2,1,0:T(8,128)(2,1)S(1)}, bf16[8,64,256]{2,1,0:T(8,128)(2,1)S(1)}, u32[]{:S(2)}, u32[]{:S(2)}) %collective-permute-start.1) | collective-permute-done | bytes 262176 | tf_op jit(solution)/shard_map/ppermute | solution.py:308
  21.9 0.1 split.3
  21.9 1.6 %collective-permute-start.3 = (bf16[4,64,256]{2,1,0:T(8,128)(2,1)S(1)}, bf16[4,64,256]{2,1,0:T(8,128)(2,1)S(1)}, u32[]{:S(2)}, u32[]{:S(2)}) collective-permute-start(bf16[4,64,256]{2,1,0:T(8,128)(2,1)S(1)} %get-tuple-element.39), channel_id=1, source_target_pairs={{0,2},{1,3},{2,0},{3,1},{4,6},{5,7},{6,4},{7,5},{8,10},{9,11},{10,... | collective-permute-start | bytes 393224 | tf_op jit(solution)/shard_map/ppermute | solution.py:308
  23.5 9.3 %collective-permute-start.2 = (bf16[2,128,1024]{2,1,0:T(8,128)(2,1)S(1)}, bf16[2,128,1024]{2,1,0:T(8,128)(2,1)S(1)}, u32[]{:S(2)}, u32[]{:S(2)}) collective-permute-start(bf16[2,128,1024]{2,1,0:T(8,128)(2,1)S(1)} %get-tuple-element.36), channel_id=1, source_target_pairs={{0,1},{1,2},{2,3},{3,4},{4,5},{5,6},{6,7},{7,8},{8,9},{9,10},{10,1... | collective-permute-start | bytes 1572872 | tf_op jit(solution)/shard_map/ppermute | solution.py:19
  32.8 0.0 collective-permute-done.3
  32.8 0.1 split.4
  32.9 5.7 %collective-permute-start.4 = (bf16[2,128,1024]{2,1,0:T(8,128)(2,1)S(1)}, bf16[2,128,1024]{2,1,0:T(8,128)(2,1)S(1)}, u32[]{:S(2)}, u32[]{:S(2)}) collective-permute-start(bf16[2,128,1024]{2,1,0:T(8,128)(2,1)S(1)} %get-tuple-element.41), channel_id=1, source_target_pairs={{0,1},{1,2},{2,3},{3,4},{4,5},{5,6},{6,7},{7,8},{8,9},{9,10},{10,1... | collective-permute-start | bytes 1572872 | tf_op jit(solution)/shard_map/ppermute | solution.py:19
  38.6 0.1 collective-permute-start.5
  38.7 7.3 %collective-permute-done.5 = bf16[2,64,256]{2,1,0:T(8,128)(2,1)S(1)} collective-permute-done((bf16[2,64,256]{2,1,0:T(8,128)(2,1)S(1)}, bf16[2,64,256]{2,1,0:T(8,128)(2,1)S(1)}, u32[]{:S(2)}, u32[]{:S(2)}) %collective-permute-start.5) | collective-permute-done | bytes 65568 | tf_op jit(solution)/shard_map/ppermute | solution.py:308
  46.0 4.0 %collective-permute-start.6 = (bf16[1,64,256]{2,1,0:T(8,128)(2,1)S(1)}, bf16[1,64,256]{2,1,0:T(8,128)(2,1)S(1)}, u32[]{:S(2)}, u32[]{:S(2)}) collective-permute-start(bf16[1,64,256]{2,1,0:T(8,128)(2,1)S(1)} %get-tuple-element.45), channel_id=1, source_target_pairs={{0,8},{1,9},{2,10},{3,11},{4,12},{5,13},{6,14},{7,15},{8,0},{9,1},... | collective-permute-start | bytes 98312 | tf_op jit(solution)/shard_map/ppermute | solution.py:308
  50.1 1.3 %lower.1.grad_in = f32[2,512,1024]{2,1,0:T(8,128)} custom-call(f32[2,8,768,128]{3,2,1,0:T(8,128)S(1)} %get-tuple-element.31.acc), custom_call_target="tpu_custom_call" | custom-call | tf_op jit(solution)/shard_map/lower/pallas_call | solution.py:403
  51.4 0.0 collective-permute-done.2.edge
  51.4 1.0 %top.1.grad_in = f32[2,512,1024]{2,1,0:T(8,128)} custom-call(f32[2,512,1024]{2,1,0:T(8,128)} %lower.1.grad_in, f32[2,8,768,128]{3,2,1,0:T(8,128)S(1)} %get-tuple-element.31.acc, bf16[2,128,1024]{2,1,0:T(8,128)(2,1)S(1)} %collective-permute-done.2.edge), custom_call_target="tpu_custom_call", output_to_operand_aliasing={{}: (0, {})} | custom-call | tf_op jit(solution)/shard_map/top/pallas_call | solution.py:413
  52.4 0.0 collective-permute-done.6
  52.4 1.0 %finish.1 = (f32[2,512,1024]{2,1,0:T(8,128)}, f32[64,256]{1,0:T(8,128)}) custom-call(f32[2,512,1024]{2,1,0:T(8,128)} %top.1.grad_in, f32[2,8,768,128]{3,2,1,0:T(8,128)S(1)} %get-tuple-element.31.acc, bf16[2,128,1024]{2,1,0:T(8,128)(2,1)S(1)} %collective-permute-done.4.edge, f32[64,256]{1,0:T(8,128)S(1)} %bitcast.15, ...), custom_call_target="tpu_custom_call", output_to_operand_aliasing={{0}: (0, {})} | custom-call | tf_op jit(solution)/shard_map/finish/pallas_call | solution.py:423
  (2 shorter events, 0.0 us)
Async XLA Ops:
  2.4 17.0 %collective-permute-start = (bf16[2,256,1024]{2,1,0:T(8,128)(2,1)S(1)}, bf16[2,256,1024]{2,1,0:T(8,128)(2,1)S(1)}, u32[]{:S(2)}, u32[]{:S(2)}) collective-permute-start(bf16[2,256,1024]{2,1,0:T(8,128)(2,1)S(1)} %slice.7), channel_id=1, source_target_pairs={{1,0},{2,1},{3,2},{4,3},{5,4},{6,5},{7,6},{8,7},{9,8},{10,9},{11,1... | collective-permute-start | bytes 3145736 | tf_op jit(solution)/shard_map/ppermute | solution.py:19
  5.6 0.7 %copy-start = (s32[1,8,2]{1,2,0:T(2,128)S(1)}, s32[1,8,2]{1,2,0:T(2,128)}, u32[]{:S(2)}) copy-start(s32[1,8,2]{1,2,0:T(2,128)} %param.9) | copy-start | bytes 196
  20.3 1.6 %collective-permute-start.1 = (bf16[8,64,256]{2,1,0:T(8,128)(2,1)S(1)}, bf16[8,64,256]{2,1,0:T(8,128)(2,1)S(1)}, u32[]{:S(2)}, u32[]{:S(2)}) collective-permute-start(bf16[8,64,256]{2,1,0:T(8,128)(2,1)S(1)} %get-tuple-element.34), channel_id=1, source_target_pairs={{0,1},{1,0},{2,3},{3,2},{4,5},{5,4},{6,7},{7,6},{8,9},{9,8},{10,11... | collective-permute-start | bytes 786440 | tf_op jit(solution)/shard_map/ppermute | solution.py:308
  21.9 10.9 %collective-permute-start.3 = (bf16[4,64,256]{2,1,0:T(8,128)(2,1)S(1)}, bf16[4,64,256]{2,1,0:T(8,128)(2,1)S(1)}, u32[]{:S(2)}, u32[]{:S(2)}) collective-permute-start(bf16[4,64,256]{2,1,0:T(8,128)(2,1)S(1)} %get-tuple-element.39), channel_id=1, source_target_pairs={{0,2},{1,3},{2,0},{3,1},{4,6},{5,7},{6,4},{7,5},{8,10},{9,11},{10,... | collective-permute-start | bytes 393224 | tf_op jit(solution)/shard_map/ppermute | solution.py:308
  23.5 27.9 %collective-permute-start.2 = (bf16[2,128,1024]{2,1,0:T(8,128)(2,1)S(1)}, bf16[2,128,1024]{2,1,0:T(8,128)(2,1)S(1)}, u32[]{:S(2)}, u32[]{:S(2)}) collective-permute-start(bf16[2,128,1024]{2,1,0:T(8,128)(2,1)S(1)} %get-tuple-element.36), channel_id=1, source_target_pairs={{0,1},{1,2},{2,3},{3,4},{4,5},{5,6},{6,7},{7,8},{8,9},{9,10},{10,1... | collective-permute-start | bytes 1572872 | tf_op jit(solution)/shard_map/ppermute | solution.py:19
  32.9 19.5 %collective-permute-start.4 = (bf16[2,128,1024]{2,1,0:T(8,128)(2,1)S(1)}, bf16[2,128,1024]{2,1,0:T(8,128)(2,1)S(1)}, u32[]{:S(2)}, u32[]{:S(2)}) collective-permute-start(bf16[2,128,1024]{2,1,0:T(8,128)(2,1)S(1)} %get-tuple-element.41), channel_id=1, source_target_pairs={{0,1},{1,2},{2,3},{3,4},{4,5},{5,6},{6,7},{7,8},{8,9},{9,10},{10,1... | collective-permute-start | bytes 1572872 | tf_op jit(solution)/shard_map/ppermute | solution.py:19
  38.6 7.4 %collective-permute-start.5 = (bf16[2,64,256]{2,1,0:T(8,128)(2,1)S(1)}, bf16[2,64,256]{2,1,0:T(8,128)(2,1)S(1)}, u32[]{:S(2)}, u32[]{:S(2)}) collective-permute-start(bf16[2,64,256]{2,1,0:T(8,128)(2,1)S(1)} %get-tuple-element.43), channel_id=1, source_target_pairs={{0,4},{1,5},{2,6},{3,7},{4,0},{5,1},{6,2},{7,3},{8,12},{9,13},{10,... | collective-permute-start | bytes 196616 | tf_op jit(solution)/shard_map/ppermute | solution.py:308
  46.0 6.4 %collective-permute-start.6 = (bf16[1,64,256]{2,1,0:T(8,128)(2,1)S(1)}, bf16[1,64,256]{2,1,0:T(8,128)(2,1)S(1)}, u32[]{:S(2)}, u32[]{:S(2)}) collective-permute-start(bf16[1,64,256]{2,1,0:T(8,128)(2,1)S(1)} %get-tuple-element.45), channel_id=1, source_target_pairs={{0,8},{1,9},{2,10},{3,11},{4,12},{5,13},{6,14},{7,15},{8,0},{9,1},... | collective-permute-start | bytes 98312 | tf_op jit(solution)/shard_map/ppermute | solution.py:308

commit v6 on v5

--- a/solution.py
+++ b/solution.py
@@ -191,7 +191,7 @@
 
 def edge_kernel(
     axis, offs, cnt, halo, obj_in, acc_in, probe_in, probe, probe_low, d_ref, dt_ref, meas_hbm,
-    obj, acc, keep, send, probe_acc,
+    obj, acc, send, probe_acc,
     counts, wave, far, grad, patch, sem_meas,
 ):
     del obj_in, acc_in, probe_in
@@ -220,16 +220,17 @@
             )
 
     mine = lax.rem(lax.axis_index(axis), 2)
-    blocks, share = keep.shape[:2]
+    blocks, share = send.shape[:2]
     flat = probe_acc.reshape(2 * blocks * share, size)
     for k in range(blocks):
-        keep[k] = flat[pl.ds(pl.multiple_of((2 * k + mine) * share, share), share), :]
         send[k] = flat[pl.ds(pl.multiple_of((2 * k + 1 - mine) * share, share), share), :].astype(
             jnp.bfloat16
         )
 
 
-def round_kernel(acc, edge_top, edge_low):
+def round_kernel(axis, acc, probe_acc, edge_top, edge_low, keep):
+    mine = lax.rem(lax.axis_index(axis), 2)
+    keep[...] = probe_acc[:, mine]
     half = edge_top.shape[1]
     start = acc.shape[2] - 2 * half
     for j in range(acc.shape[1]):
@@ -372,33 +373,33 @@
     )(scan_offsets, scan_counts, object_hbm, probe, d_mat, dt_mat, measured)
     devices = lax.axis_size("tr")
     shares = (devices // 2, 2 * modes * size // devices, size)
-    _, acc, keep, send, _ = pl.pallas_call(
+    _, acc, send, probe_acc = pl.pallas_call(
         functools.partial(edge_kernel, "tr"),
         out_shape=(
             tall,
             tall,
-            jax.ShapeDtypeStruct(shares, f32),
             jax.ShapeDtypeStruct(shares, bf16),
             planes,
         ),
         in_specs=[smem, smem] + [vmem] * 8 + [hbm],
-        out_specs=(vmem,) * 5,
+        out_specs=(vmem,) * 4,
         scratch_shapes=work + [pltpu.SemaphoreType.DMA((slots,))],
-        input_output_aliases={3: 0, 4: 1, 5: 4},
+        input_output_aliases={3: 0, 4: 1, 5: 3},
         compiler_params=params,
         cost_estimate=cost,
         name="edge",
     )(scan_offsets, scan_counts, halo, obj, acc, probe_acc, probe, probe_low, d_mat, dt_mat, measured)
     small = pltpu.CompilerParams(vmem_limit_bytes=8 * 1024 * 1024)
-    edge_top, edge_low = pl.pallas_call(
-        round_kernel,
-        out_shape=(jax.ShapeDtypeStruct((2, size // 2, cols), bf16),) * 2,
-        in_specs=[vmem],
-        out_specs=(vmem,) * 2,
+    edge_top, edge_low, keep = pl.pallas_call(
+        functools.partial(round_kernel, "tr"),
+        out_shape=(jax.ShapeDtypeStruct((2, size // 2, cols), bf16),) * 2
+        + (jax.ShapeDtypeStruct(shares, f32),),
+        in_specs=[vmem] * 2,
+        out_specs=(vmem,) * 3,
         compiler_params=small,
         cost_estimate=pl.CostEstimate(flops=1 << 19, bytes_accessed=3 << 20, transcendentals=0),
         name="rounding",
-    )(acc)
+    )(acc, probe_acc.reshape(shares[0], 2, *shares[1:]))
     own, other, edges = reduce_and_pass_edges(keep, send, (edge_top, edge_low), "tr", small)
     grad = pl.pallas_call(
         lower_kernel,

time: 53.7 us -> 53.6 us (level)
  no operation moved by 1% of the time
where the time goes in v6:
time: 53.6 us; the launch traced here: 53.4 us
  starting transfers between devices  23.4 us (44%)
  waiting for transfers between devices  15.9 us (30%)
  Pallas kernels  10.2 us (19%)
  local copies, waits for them, and re-layouts  2.42 us (5%)
  between operations  1.42 us (3%)
    ppermute x3, starting transfers between devices, shifted(): lax.ppermute(value, axis, [(source, source + steps) for source in range(i...  17.6 us
    ppermute x4, waiting for transfers between devices, reduce_and_pass_edges(): got = lax.ppermute(send, axis, [(s, s ^ bit) for s in range(devices)])  8.53 us
    ppermute x3, waiting for transfers between devices, shifted(): lax.ppermute(value, axis, [(source, source + steps) for source in range(i...  7.4 us
    ppermute x4, starting transfers between devices, reduce_and_pass_edges(): got = lax.ppermute(send, axis, [(s, s ^ bit) for s in range(devices)])  5.76 us
    pallas_call x1, Pallas kernels, gradients(): pl.pallas_call(inner_kernel, out_shape=(tall, tall, planes, planes, squar...  5.7 us
    slice x1, local copies, waits for them, and re-layouts, gradients(): halo = shifted(object_field[:, :size, :].astype(jnp.bfloat16), 'tr', -1)  1.75 us
    pallas_call x1, Pallas kernels, gradients(): pl.pallas_call(lower_kernel, out_shape=jax.ShapeDtypeStruct(object_field....  1.31 us
  transfers between devices with their start and end apart: 7, of which 3 were waited for; matrix products, arithmetic and copies ran while one was open for 0% of the time, Pallas kernels for 16%

profile of v6, /device:TPU:15, one launch (start us, length us, event | category | flops | bytes accessed | tf_op | source)
XLA Modules:
  0.0 53.4 jit_solution(1613593693202036183)
XLA Ops:
  0.6 1.7 %slice.7 = bf16[2,256,1024]{2,1,0:T(8,128)(2,1)S(1)} slice(f32[2,512,1024]{2,1,0:T(8,128)} %obj_hbm.1), slice={[0:2], [0:256], [0:1024]} | slice | bytes 2097152 | tf_op jit(solution)/shard_map/slice | solution.py:339
  2.4 2.6 %collective-permute-start = (bf16[2,256,1024]{2,1,0:T(8,128)(2,1)S(1)}, bf16[2,256,1024]{2,1,0:T(8,128)(2,1)S(1)}, u32[]{:S(2)}, u32[]{:S(2)}) collective-permute-start(bf16[2,256,1024]{2,1,0:T(8,128)(2,1)S(1)} %slice.7), channel_id=1, source_target_pairs={{1,0},{2,1},{3,2},{4,3},{5,4},{6,5},{7,6},{8,7},{9,8},{10,9},{11,1... | collective-permute-start | bytes 3145736 | tf_op jit(solution)/shard_map/ppermute | solution.py:19
  5.6 0.0 copy-start
  5.6 0.7 %copy-done = s32[1,8,2]{1,2,0:T(2,128)S(1)} copy-done((s32[1,8,2]{1,2,0:T(2,128)S(1)}, s32[1,8,2]{1,2,0:T(2,128)}, u32[]{:S(2)}) %copy-start) | copy-done | bytes 88
  6.3 5.7 %inner.1 = (f32[2,8,768,128]{3,2,1,0:T(8,128)S(1)}, f32[2,8,768,128]{3,2,1,0:T(8,128)S(1)}, f32[4,256,256]{2,1,0:T(8,128)S(1)}, f32[4,256,256]{2,1,0:T(8,128)S(1...) custom-call(s32[1,2,8]{2,1,0:T(2,128)S(1)} %bitcast.20, ...), custom_call_target="tpu_custom_call" | custom-call | flops 8589934592 | bytes 8388608 | tf_op jit(solution)/shard_map/inner/pallas_call | solution.py:364
  12.0 7.4 %collective-permute-done.halo = bf16[2,256,1024]{2,1,0:T(8,128)(2,1)S(1)} collective-permute-done((bf16[2,256,1024]{2,1,0:T(8,128)(2,1)S(1)}, bf16[2,256,1024]{2,1,0:T(8,128)(2,1)S(1)}, u32[]{:S(2)}, u32[]{:S(2)}) %collective-permute-start) | collective-permute-done | bytes 1048608 | tf_op jit(solution)/shard_map/ppermute | solution.py:19
  19.4 0.8 %edge.1 = (f32[2,8,768,128]{3,2,1,0:T(8,128)S(1)}, f32[2,8,768,128]{3,2,1,0:T(8,128)S(1)}, bf16[8,64,256]{2,1,0:T(8,128)(2,1)S(1)}, f32[4,256,256]{2,1,0:T(8,128)S(1)}) custom-call(s32[1,2,8]{2,1,0:T(2,128)S(1)} %bitcast.21, s32[1]{0:T(128)S(6)} %copy.19.cnt, ...), custom_call_target="tpu_custom_call", output_to_operand_aliasing={{0}: (3, {}), {1}: (4, {}), {3}: (5, {})} | custom-call | flops 8589934592 | bytes 8388608 | tf_op jit(solution)/shard_map/edge/pallas_call | solution.py:376
  20.2 0.1 collective-permute-start.1
  20.3 0.3 rounding.1
  20.6 1.2 %collective-permute-done.1 = bf16[8,64,256]{2,1,0:T(8,128)(2,1)S(1)} collective-permute-done((bf16[8,64,256]{2,1,0:T(8,128)(2,1)S(1)}, bf16[8,64,256]{2,1,0:T(8,128)(2,1)S(1)}, u32[]{:S(2)}, u32[]{:S(2)}) %collective-permute-start.1) | collective-permute-done | bytes 262176 | tf_op jit(solution)/shard_map/ppermute | solution.py:309
  21.9 1.6 %collective-permute-start.3 = (bf16[4,64,256]{2,1,0:T(8,128)(2,1)S(1)}, bf16[4,64,256]{2,1,0:T(8,128)(2,1)S(1)}, u32[]{:S(2)}, u32[]{:S(2)}) collective-permute-start(bf16[4,64,256]{2,1,0:T(8,128)(2,1)S(1)} %get-tuple-element.41), channel_id=1, source_target_pairs={{0,2},{1,3},{2,0},{3,1},{4,6},{5,7},{6,4},{7,5},{8,10},{9,11},{10,... | collective-permute-start | bytes 393224 | tf_op jit(solution)/shard_map/ppermute | solution.py:309
  23.4 9.3 %collective-permute-start.2 = (bf16[2,128,1024]{2,1,0:T(8,128)(2,1)S(1)}, bf16[2,128,1024]{2,1,0:T(8,128)(2,1)S(1)}, u32[]{:S(2)}, u32[]{:S(2)}) collective-permute-start(bf16[2,128,1024]{2,1,0:T(8,128)(2,1)S(1)} %get-tuple-element.38), channel_id=1, source_target_pairs={{0,1},{1,2},{2,3},{3,4},{4,5},{5,6},{6,7},{7,8},{8,9},{9,10},{10,1... | collective-permute-start | bytes 1572872 | tf_op jit(solution)/shard_map/ppermute | solution.py:19
  32.8 0.0 collective-permute-done.3
  32.8 5.7 %collective-permute-start.4 = (bf16[2,128,1024]{2,1,0:T(8,128)(2,1)S(1)}, bf16[2,128,1024]{2,1,0:T(8,128)(2,1)S(1)}, u32[]{:S(2)}, u32[]{:S(2)}) collective-permute-start(bf16[2,128,1024]{2,1,0:T(8,128)(2,1)S(1)} %get-tuple-element.43), channel_id=1, source_target_pairs={{0,1},{1,2},{2,3},{3,4},{4,5},{5,6},{6,7},{7,8},{8,9},{9,10},{10,1... | collective-permute-start | bytes 1572872 | tf_op jit(solution)/shard_map/ppermute | solution.py:19
  38.5 0.1 collective-permute-start.5
  38.6 7.3 %collective-permute-done.5 = bf16[2,64,256]{2,1,0:T(8,128)(2,1)S(1)} collective-permute-done((bf16[2,64,256]{2,1,0:T(8,128)(2,1)S(1)}, bf16[2,64,256]{2,1,0:T(8,128)(2,1)S(1)}, u32[]{:S(2)}, u32[]{:S(2)}) %collective-permute-start.5) | collective-permute-done | bytes 65568 | tf_op jit(solution)/shard_map/ppermute | solution.py:309
  46.0 4.1 %collective-permute-start.6 = (bf16[1,64,256]{2,1,0:T(8,128)(2,1)S(1)}, bf16[1,64,256]{2,1,0:T(8,128)(2,1)S(1)}, u32[]{:S(2)}, u32[]{:S(2)}) collective-permute-start(bf16[1,64,256]{2,1,0:T(8,128)(2,1)S(1)} %get-tuple-element.47), channel_id=1, source_target_pairs={{0,8},{1,9},{2,10},{3,11},{4,12},{5,13},{6,14},{7,15},{8,0},{9,1},... | collective-permute-start | bytes 98312 | tf_op jit(solution)/shard_map/ppermute | solution.py:309
  50.0 1.3 %lower.1.grad_in = f32[2,512,1024]{2,1,0:T(8,128)} custom-call(f32[2,8,768,128]{3,2,1,0:T(8,128)S(1)} %get-tuple-element.32.acc), custom_call_target="tpu_custom_call" | custom-call | tf_op jit(solution)/shard_map/lower/pallas_call | solution.py:404
  51.3 0.0 collective-permute-done.2.edge
  51.3 1.0 %top.1.grad_in = f32[2,512,1024]{2,1,0:T(8,128)} custom-call(f32[2,512,1024]{2,1,0:T(8,128)} %lower.1.grad_in, f32[2,8,768,128]{3,2,1,0:T(8,128)S(1)} %get-tuple-element.32.acc, bf16[2,128,1024]{2,1,0:T(8,128)(2,1)S(1)} %collective-permute-done.2.edge), custom_call_target="tpu_custom_call", output_to_operand_aliasing={{}: (0, {})} | custom-call | tf_op jit(solution)/shard_map/top/pallas_call | solution.py:414
  52.3 0.0 collective-permute-done.6
  52.4 0.0 collective-permute-done.4.edge
  52.4 1.0 %finish.1 = (f32[2,512,1024]{2,1,0:T(8,128)}, f32[64,256]{1,0:T(8,128)}) custom-call(f32[2,512,1024]{2,1,0:T(8,128)} %top.1.grad_in, f32[2,8,768,128]{3,2,1,0:T(8,128)S(1)} %get-tuple-element.32.acc, bf16[2,128,1024]{2,1,0:T(8,128)(2,1)S(1)} %collective-permute-done.4.edge, f32[64,256]{1,0:T(8,128)S(1)} %bitcast.17, ...), custom_call_target="tpu_custom_call", output_to_operand_aliasing={{0}: (0, {})} | custom-call | tf_op jit(solution)/shard_map/finish/pallas_call | solution.py:424
  (3 shorter events, 0.1 us)
Async XLA Ops:
  2.4 17.0 %collective-permute-start = (bf16[2,256,1024]{2,1,0:T(8,128)(2,1)S(1)}, bf16[2,256,1024]{2,1,0:T(8,128)(2,1)S(1)}, u32[]{:S(2)}, u32[]{:S(2)}) collective-permute-start(bf16[2,256,1024]{2,1,0:T(8,128)(2,1)S(1)} %slice.7), channel_id=1, source_target_pairs={{1,0},{2,1},{3,2},{4,3},{5,4},{6,5},{7,6},{8,7},{9,8},{10,9},{11,1... | collective-permute-start | bytes 3145736 | tf_op jit(solution)/shard_map/ppermute | solution.py:19
  5.6 0.7 %copy-start = (s32[1,8,2]{1,2,0:T(2,128)S(1)}, s32[1,8,2]{1,2,0:T(2,128)}, u32[]{:S(2)}) copy-start(s32[1,8,2]{1,2,0:T(2,128)} %param.9) | copy-start | bytes 196
  20.2 1.6 %collective-permute-start.1 = (bf16[8,64,256]{2,1,0:T(8,128)(2,1)S(1)}, bf16[8,64,256]{2,1,0:T(8,128)(2,1)S(1)}, u32[]{:S(2)}, u32[]{:S(2)}) collective-permute-start(bf16[8,64,256]{2,1,0:T(8,128)(2,1)S(1)} %get-tuple-element.36), channel_id=1, source_target_pairs={{0,1},{1,0},{2,3},{3,2},{4,5},{5,4},{6,7},{7,6},{8,9},{9,8},{10,11... | collective-permute-start | bytes 786440 | tf_op jit(solution)/shard_map/ppermute | solution.py:309
  21.9 10.9 %collective-permute-start.3 = (bf16[4,64,256]{2,1,0:T(8,128)(2,1)S(1)}, bf16[4,64,256]{2,1,0:T(8,128)(2,1)S(1)}, u32[]{:S(2)}, u32[]{:S(2)}) collective-permute-start(bf16[4,64,256]{2,1,0:T(8,128)(2,1)S(1)} %get-tuple-element.41), channel_id=1, source_target_pairs={{0,2},{1,3},{2,0},{3,1},{4,6},{5,7},{6,4},{7,5},{8,10},{9,11},{10,... | collective-permute-start | bytes 393224 | tf_op jit(solution)/shard_map/ppermute | solution.py:309
  23.4 27.9 %collective-permute-start.2 = (bf16[2,128,1024]{2,1,0:T(8,128)(2,1)S(1)}, bf16[2,128,1024]{2,1,0:T(8,128)(2,1)S(1)}, u32[]{:S(2)}, u32[]{:S(2)}) collective-permute-start(bf16[2,128,1024]{2,1,0:T(8,128)(2,1)S(1)} %get-tuple-element.38), channel_id=1, source_target_pairs={{0,1},{1,2},{2,3},{3,4},{4,5},{5,6},{6,7},{7,8},{8,9},{9,10},{10,1... | collective-permute-start | bytes 1572872 | tf_op jit(solution)/shard_map/ppermute | solution.py:19
  32.8 19.5 %collective-permute-start.4 = (bf16[2,128,1024]{2,1,0:T(8,128)(2,1)S(1)}, bf16[2,128,1024]{2,1,0:T(8,128)(2,1)S(1)}, u32[]{:S(2)}, u32[]{:S(2)}) collective-permute-start(bf16[2,128,1024]{2,1,0:T(8,128)(2,1)S(1)} %get-tuple-element.43), channel_id=1, source_target_pairs={{0,1},{1,2},{2,3},{3,4},{4,5},{5,6},{6,7},{7,8},{8,9},{9,10},{10,1... | collective-permute-start | bytes 1572872 | tf_op jit(solution)/shard_map/ppermute | solution.py:19
  38.5 7.4 %collective-permute-start.5 = (bf16[2,64,256]{2,1,0:T(8,128)(2,1)S(1)}, bf16[2,64,256]{2,1,0:T(8,128)(2,1)S(1)}, u32[]{:S(2)}, u32[]{:S(2)}) collective-permute-start(bf16[2,64,256]{2,1,0:T(8,128)(2,1)S(1)} %get-tuple-element.45), channel_id=1, source_target_pairs={{0,4},{1,5},{2,6},{3,7},{4,0},{5,1},{6,2},{7,3},{8,12},{9,13},{10,... | collective-permute-start | bytes 196616 | tf_op jit(solution)/shard_map/ppermute | solution.py:309
  46.0 6.4 %collective-permute-start.6 = (bf16[1,64,256]{2,1,0:T(8,128)(2,1)S(1)}, bf16[1,64,256]{2,1,0:T(8,128)(2,1)S(1)}, u32[]{:S(2)}, u32[]{:S(2)}) collective-permute-start(bf16[1,64,256]{2,1,0:T(8,128)(2,1)S(1)} %get-tuple-element.47), channel_id=1, source_target_pairs={{0,8},{1,9},{2,10},{3,11},{4,12},{5,13},{6,14},{7,15},{8,0},{9,1},... | collective-permute-start | bytes 98312 | tf_op jit(solution)/shard_map/ppermute | solution.py:309
